TPU v7x, 1024 devices: a whole 8x8x8 slice. The times are simulated.
1024 devices in a mesh: gy: 64 (over y, z), gz: 16 (over x, core).
Axes of the slice: x: 8, y: 8, z: 8, core: 2. Of those that a mesh axis runs over, the one named last changes fastest.
Arguments:
- velocity: float32 [3, 2, 4096, 4096], P(None, None, 'gy', 'gz'), may hold values from -6 to 6
Outputs:
- deriv_y: float32 [3, 2, 4096, 4096], P(None, None, 'gy', 'gz')
- deriv_z: float32 [3, 2, 4096, 4096], P(None, None, 'gy', 'gz')
All inputs are finite; a program needn't handle non-finite values.
Results may differ from a plain program's by a relative error of at most 0.00007.
Values sent between devices are 32-bit elements; how exact they have to be, the bound alone decides.
No kernel may reach another device: no remote copies, remote signals or barrier semaphores. Data moves between devices by JAX's collectives and lax.ppermute only.
A program may use at most 32 MiB of HBM per device.

v0:
```python
import math

import jax
import jax.numpy as jnp
from jax import lax
from jax.sharding import PartitionSpec as P

coef_near = 7.0 / 9.0
coef_far = 1.0 / 36.0
alpha_side = 1.0 / 3.0
ratio_root = 1.5 - math.sqrt(5.0) / 2.0
margin_cells = 24
best = lax.Precision.HIGHEST


def padded_2(block, sides, width):
    for axis, dim in sides:
        count = lax.axis_size(axis)
        forward = [(i, i + 1) for i in range(count - 1)]
        forward.append((count - 1, 0))
        backward = [(target, source) for source, target in forward]
        low = lax.ppermute(
            lax.slice_in_dim(block, block.shape[dim] - width, None, axis=dim), axis, forward
        )
        high = lax.ppermute(lax.slice_in_dim(block, 0, width, axis=dim), axis, backward)
        block = jnp.concatenate([low, block, high], axis=dim)
    return block


def shifted(shard, axis, by):
    count = lax.axis_size(axis)
    return lax.ppermute(shard, axis, [(i, (i + by) % count) for i in range(count)])


def alternating(power):
    signs = jnp.where(power % 2 == 0, 1.0, -1.0).astype(jnp.float32)
    return signs * jnp.power(jnp.float32(ratio_root), power.astype(jnp.float32))


def explicit(padded, axis):
    length = padded.shape[axis] - 4

    def part(start):
        return lax.slice_in_dim(padded, start, start + length, axis=axis)

    return coef_near * (part(3) - part(1)) + coef_far * (part(4) - part(0))


def green_window(count):
    rows = jnp.arange(count, dtype=jnp.int32)[:, None]
    cols = jnp.arange(count + 2 * margin_cells, dtype=jnp.int32)[None, :]
    spread = jnp.abs(rows + margin_cells - cols)
    scale = ratio_root / alpha_side / (1.0 - ratio_root * ratio_root)
    return scale * alternating(spread)


def y_chain(velocity):
    count = velocity.shape[2]
    padded = padded_2(velocity, (("gy", 2),), 2)
    rhs_rows = explicit(padded, 2)
    rows = jnp.arange(count, dtype=jnp.int32)[:, None]
    cols = jnp.arange(count, dtype=jnp.int32)[None, :]
    distance = jnp.abs(rows - cols)
    lower = jnp.where(rows >= cols, ratio_root / alpha_side * alternating(distance), 0.0)
    upper = jnp.where(cols >= rows, alternating(distance), 0.0)
    places = jnp.arange(count, dtype=jnp.int32)
    head_decay = alternating(places + 1)
    tail_decay = alternating(count - places)
    forward = jnp.einsum("ij,cxjz->cxiz", lower, rhs_rows, precision=best)
    carry_in = shifted(forward[:, :, -1, :], "gy", 1)
    forward = forward + head_decay[None, None, :, None] * carry_in[:, :, None, :]
    backward = jnp.einsum("ij,cxjz->cxiz", upper, forward, precision=best)
    carry_back = shifted(backward[:, :, 0, :], "gy", -1)
    return backward + tail_decay[None, None, :, None] * carry_back[:, :, None, :]


def z_regroup(velocity):
    block = velocity.shape[3]
    window = green_window(block)
    left_part = window[:, :margin_cells]
    center = window[:, margin_cells : margin_cells + block]
    right_part = window[:, margin_cells + block :]
    line = lax.all_to_all(velocity, "gz", split_axis=2, concat_axis=3, tiled=True)
    rhs_line = coef_near * (jnp.roll(line, -1, axis=3) - jnp.roll(line, 1, axis=3))
    rhs_line = rhs_line + coef_far * (jnp.roll(line, -2, axis=3) - jnp.roll(line, 2, axis=3))
    shape_in = rhs_line.shape
    blocks = rhs_line.reshape(shape_in[0], shape_in[1], shape_in[2], shape_in[3] // block, block)
    before = jnp.roll(blocks, 1, axis=3)[..., block - margin_cells :]
    after = jnp.roll(blocks, -1, axis=3)[..., :margin_cells]
    result = jnp.einsum("ij,cxybj->cxybi", center, blocks, precision=best)
    result = result + jnp.einsum("ij,cxybj->cxybi", left_part, before, precision=best)
    result = result + jnp.einsum("ij,cxybj->cxybi", right_part, after, precision=best)
    result = result.reshape(shape_in)
    return lax.all_to_all(result, "gz", split_axis=3, concat_axis=2, tiled=True)


def per_device(velocity):
    deriv_y = y_chain(velocity)
    deriv_z = z_regroup(velocity)
    return (deriv_y, deriv_z)


def solution(mesh):
    in_specs = (P(None, None, "gy", "gz"),)
    out_specs = (P(None, None, "gy", "gz"), P(None, None, "gy", "gz"))
    return jax.shard_map(
        per_device, mesh=mesh, in_specs=in_specs, out_specs=out_specs, check_vma=False
    )
```

profile of v0, /device:TPU:1, one launch (start us, length us, event | category | flops | bytes accessed | tf_op | source)
XLA Modules:
  0.0 133.9 jit_solution(13524486298522021622)
XLA Ops:
  0.6 2.1 %copy.12 = f32[3,2,64,256]{3,0,1,2:T(4,128)} copy(f32[3,2,64,256]{3,2,1,0:T(8,128)} %param.1) | data formatting | bytes 786432 | tf_op args[0]
  2.7 17.5 %all-to-all-start = ((f32[3,2,64,256]{3,0,1,2:T(4,128)}), f32[3,2,64,256]{3,0,1,2:T(4,128)S(1)}, u32[]{:S(2)}, u32[]{:S(2)}) async-start(f32[3,2,64,256]{3,0,1,2:T(4,128)} %copy.12), calls=%async_computation | async-start | bytes 1048576 | tf_op jit(solution)/shard_map/all_to_all | solution.py:83
  20.2 0.8 fusion.79
  21.0 11.5 %collective-permute-start = (f32[3,2,2,256]{3,2,1,0:T(2,128)S(1)}, f32[3,2,2,256]{3,2,1,0:T(2,128)S(1)}, u32[]{:S(2)}, u32[]{:S(2)}) collective-permute-start(f32[3,2,2,256]{3,2,1,0:T(2,128)S(1)} %get-tuple-element.14), channel_id=1, source_target_pairs={{16,0},{32,16},{48,32},{64,48},{80,64},{96,80},{112,96},{128,112},... | collective-permute-start | bytes 36872 | tf_op jit(solution)/shard_map/ppermute | solution.py:25
  32.6 1.9 %collective-permute-start.1 = (f32[3,2,2,256]{3,2,1,0:T(2,128)S(1)}, f32[3,2,2,256]{3,2,1,0:T(2,128)S(1)}, u32[]{:S(2)}, u32[]{:S(2)}) collective-permute-start(f32[3,2,2,256]{3,2,1,0:T(2,128)S(1)} %get-tuple-element.15), channel_id=1, source_target_pairs={{0,16},{16,32},{32,48},{48,64},{64,80},{80,96},{96,112},{112,128},... | collective-permute-start | bytes 36872 | tf_op jit(solution)/shard_map/ppermute | solution.py:22
  34.5 0.4 multiply_multiply_fusion
  34.9 1.0 constant_dynamic-update-slice_fusion.1
  35.9 0.0 collective-permute-done
  36.0 1.6 %all-to-all-done = f32[3,2,64,256]{3,0,1,2:T(4,128)S(1)} async-done(((f32[3,2,64,256]{3,0,1,2:T(4,128)}), f32[3,2,64,256]{3,0,1,2:T(4,128)S(1)}, u32[]{:S(2)}, u32[]{:S(2)}) %all-to-all-start) | async-done | bytes 393248 | tf_op jit(solution)/shard_map/all_to_all | solution.py:83
  37.6 0.2 copy.13
  37.8 0.2 all_to_all.29
  38.0 0.3 fusion.78
  38.3 0.3 fusion.76
  38.5 0.1 fusion.77
  38.6 0.1 fusion.75
  38.7 0.5 fusion.14
  39.2 0.3 add.94
  39.5 0.1 fusion.73
  39.6 0.6 fusion.18
  40.2 0.5 convolution_add_fusion.1
  40.7 0.6 convolution_add_fusion
  41.3 0.0 copy-start
  41.3 9.1 %copy.25 = f32[3,2,4,16,256]{2,1,0,4,3:T(2,128)} copy(f32[3,2,4,16,256]{4,3,2,1,0:T(8,128)S(1)} %convolution_add_fusion) | data formatting | bytes 786432 | tf_op jit(solution)/shard_map/reshape | solution.py:93
  50.3 17.6 %reshape.72 = f32[16,1,6144]{2,1,0:T(1,128)} reshape(f32[4096,3,2,4]{3,2,1,0:T(2,128)} %bitcast.43) | data formatting | bytes 786432
  67.9 5.9 %all-to-all-start.1 = ((f32[16,1,6144]{2,1,0:T(1,128)}), f32[16,1,6144]{2,1,0:T(1,128)S(1)}, u32[]{:S(2)}, u32[]{:S(2)}) async-start(f32[16,1,6144]{2,1,0:T(1,128)} %reshape.72), calls=%async_computation.1 | async-start | bytes 786432 | tf_op jit(solution)/shard_map/all_to_all | solution.py:94
  73.8 0.0 collective-permute-done.1
  73.8 0.0 copy-done
  73.9 0.7 convolution_bitcast_fusion.1
  74.6 1.9 %collective-permute-start.2 = (f32[3,2,256]{2,1,0:T(2,128)S(1)}, f32[3,2,256]{2,1,0:T(2,128)S(1)}, u32[]{:S(2)}, u32[]{:S(2)}) collective-permute-start(f32[3,2,256]{2,1,0:T(2,128)S(1)} %bitcast.46), channel_id=1, source_target_pairs={{0,16},{16,32},{32,48},{48,64},{64,80},{80,96},{96,112},{112,128},... | collective-permute-start | bytes 18440 | tf_op jit(solution)/shard_map/ppermute | solution.py:32
  76.5 8.1 %collective-permute-done.2 = f32[3,2,256]{2,1,0:T(2,128)S(1)} collective-permute-done((f32[3,2,256]{2,1,0:T(2,128)S(1)}, f32[3,2,256]{2,1,0:T(2,128)S(1)}, u32[]{:S(2)}, u32[]{:S(2)}) %collective-permute-start.2) | collective-permute-done | bytes 6176 | tf_op jit(solution)/shard_map/ppermute | solution.py:32
  84.7 0.6 convolution_bitcast_fusion
  85.3 3.9 %collective-permute-start.3 = (f32[3,2,256]{2,1,0:T(2,128)S(1)}, f32[3,2,256]{2,1,0:T(2,128)S(1)}, u32[]{:S(2)}, u32[]{:S(2)}) collective-permute-start(f32[3,2,256]{2,1,0:T(2,128)S(1)} %bitcast.47), channel_id=1, source_target_pairs={{0,1008},{16,0},{32,16},{48,32},{64,48},{80,64},{96,80},{112,96},{... | collective-permute-start | bytes 18440 | tf_op jit(solution)/shard_map/ppermute | solution.py:32
  89.2 0.6 collective-permute-done.3
  89.7 0.8 multiply_add_fusion
  90.6 0.0 all-to-all-done.1
  90.6 0.5 broadcast.146
  91.1 1.6 %reduce = f32[16,6144]{1,0:T(8,128)S(1)} reduce(f32[16,1,6144]{2,1,0:T(1,128)S(1)} %all-to-all-done.1, f32[]{:T(128)} %broadcast.146), dimensions={1}, to_apply=%all_to_all.30.reduce_sub_computation | reduce | bytes 786436 | tf_op jit(solution)/shard_map/all_to_all | solution.py:94
  92.7 24.8 %reshape.73 = f32[4096,3,2,4]{3,2,1,0:T(2,128)} reshape(f32[16,6144]{1,0:T(8,128)S(1)} %reduce) | data formatting | bytes 786432
  117.5 15.5 %copy.17 = f32[3,2,16,4,256]{4,3,2,1,0:T(4,128)S(1)} copy(f32[3,2,16,4,256]{3,1,0,4,2:T(2,128)} %bitcast.44) | data formatting | bytes 786432 | tf_op jit(solution)/shard_map/all_to_all | solution.py:94
  133.0 0.9 all_to_all.33
  (9 shorter events, 0.1 us)
Async XLA Ops:
  2.7 34.9 %all-to-all-start = ((f32[3,2,64,256]{3,0,1,2:T(4,128)}), f32[3,2,64,256]{3,0,1,2:T(4,128)S(1)}, u32[]{:S(2)}, u32[]{:S(2)}) async-start(f32[3,2,64,256]{3,0,1,2:T(4,128)} %copy.12), calls=%async_computation | async-start | bytes 1048576 | tf_op jit(solution)/shard_map/all_to_all | solution.py:83
  21.0 14.9 %collective-permute-start = (f32[3,2,2,256]{3,2,1,0:T(2,128)S(1)}, f32[3,2,2,256]{3,2,1,0:T(2,128)S(1)}, u32[]{:S(2)}, u32[]{:S(2)}) collective-permute-start(f32[3,2,2,256]{3,2,1,0:T(2,128)S(1)} %get-tuple-element.14), channel_id=1, source_target_pairs={{16,0},{32,16},{48,32},{64,48},{80,64},{96,80},{112,96},{128,112},... | collective-permute-start | bytes 36872 | tf_op jit(solution)/shard_map/ppermute | solution.py:25
  32.6 41.3 %collective-permute-start.1 = (f32[3,2,2,256]{3,2,1,0:T(2,128)S(1)}, f32[3,2,2,256]{3,2,1,0:T(2,128)S(1)}, u32[]{:S(2)}, u32[]{:S(2)}) collective-permute-start(f32[3,2,2,256]{3,2,1,0:T(2,128)S(1)} %get-tuple-element.15), channel_id=1, source_target_pairs={{0,16},{16,32},{32,48},{48,64},{64,80},{80,96},{96,112},{112,128},... | collective-permute-start | bytes 36872 | tf_op jit(solution)/shard_map/ppermute | solution.py:22
  41.3 32.6 %copy-start = (f32[3,2,64,256]{3,2,1,0:T(8,128)S(1)}, f32[3,2,64,256]{3,2,1,0:T(8,128)}, u32[]{:S(2)}) copy-start(f32[3,2,64,256]{3,2,1,0:T(8,128)} %param.1) | copy-start | bytes 1179652
  67.9 22.6 %all-to-all-start.1 = ((f32[16,1,6144]{2,1,0:T(1,128)}), f32[16,1,6144]{2,1,0:T(1,128)S(1)}, u32[]{:S(2)}, u32[]{:S(2)}) async-start(f32[16,1,6144]{2,1,0:T(1,128)} %reshape.72), calls=%async_computation.1 | async-start | bytes 786432 | tf_op jit(solution)/shard_map/all_to_all | solution.py:94
  74.6 10.1 %collective-permute-start.2 = (f32[3,2,256]{2,1,0:T(2,128)S(1)}, f32[3,2,256]{2,1,0:T(2,128)S(1)}, u32[]{:S(2)}, u32[]{:S(2)}) collective-permute-start(f32[3,2,256]{2,1,0:T(2,128)S(1)} %bitcast.46), channel_id=1, source_target_pairs={{0,16},{16,32},{32,48},{48,64},{64,80},{80,96},{96,112},{112,128},... | collective-permute-start | bytes 18440 | tf_op jit(solution)/shard_map/ppermute | solution.py:32
  85.3 4.5 %collective-permute-start.3 = (f32[3,2,256]{2,1,0:T(2,128)S(1)}, f32[3,2,256]{2,1,0:T(2,128)S(1)}, u32[]{:S(2)}, u32[]{:S(2)}) collective-permute-start(f32[3,2,256]{2,1,0:T(2,128)S(1)} %bitcast.47), channel_id=1, source_target_pairs={{0,1008},{16,0},{32,16},{48,32},{64,48},{80,64},{96,80},{112,96},{... | collective-permute-start | bytes 18440 | tf_op jit(solution)/shard_map/ppermute | solution.py:32
where the time goes:
time: 135 us; the launch traced here: 134 us
  local copies, waits for them, and re-layouts  73.8 us (55%)
  starting transfers between devices  42.7 us (32%)
  waiting for transfers between devices  10.3 us (8%)
  other arithmetic  3.31 us (2%)
  matrix products  2.93 us (2%)
    unnamed x8, local copies, waits for them, and re-layouts  45.5 us
    all_to_all x1, starting transfers between devices, z_regroup(): lax.all_to_all(velocity, 'gz', split_axis=2, concat_axis=3, tiled=True)  17.5 us
    all_to_all x3, local copies, waits for them, and re-layouts, z_regroup(): return lax.all_to_all(result, 'gz', split_axis=3, concat_axis=2, tiled=True)  16.9 us
    ppermute x1, starting transfers between devices, padded_2(): lax.ppermute(lax.slice_in_dim(block, 0, width, axis=dim), axis, backward)  11.5 us
    reshape x1, local copies, waits for them, and re-layouts, z_regroup(): result = result.reshape(shape_in)  9.05 us
    ppermute x2, waiting for transfers between devices, shifted(): lax.ppermute(shard, axis, [(i, (i + by) % count) for i in range(count)])  8.69 us
    all_to_all x1, starting transfers between devices, z_regroup(): return lax.all_to_all(result, 'gz', split_axis=3, concat_axis=2, tiled=True)  5.9 us
    ppermute x2, starting transfers between devices, shifted(): lax.ppermute(shard, axis, [(i, (i + by) % count) for i in range(count)])  5.81 us
  transfers between devices with their start and end apart: 6, of which 3 were waited for; matrix products, arithmetic and copies ran while one was open for 26% of the time, Pallas kernels for 0%

commit v1 on v0

v1 whole, which is shorter than its diff:
```python
import math

import jax
import jax.numpy as jnp
import numpy as np
from jax import lax
from jax.sharding import PartitionSpec as P

best = lax.Precision.HIGHEST


def response(lags):
    root = 1.5 - math.sqrt(5.0) / 2.0
    scale = root * 3.0 / (1.0 - root * root)

    def green(n):
        n = np.abs(n)
        return scale * np.where(n % 2 == 0, 1.0, -1.0) * root ** n.astype(np.float64)

    n = np.asarray(lags)
    near = 7.0 / 9.0 * (green(n + 1) - green(n - 1))
    far = 1.0 / 36.0 * (green(n + 2) - green(n - 2))
    return near + far


def operator(rows, cols):
    return response(np.asarray(rows)[:, None] - np.asarray(cols)[None, :])


def tails(count):
    root = 1.5 - math.sqrt(5.0) / 2.0
    cells = np.arange(count)
    low = np.zeros((count, 2))
    low[0, 0] = 1.0
    low[1:, 1] = (-root) ** (cells[1:] - 1.0)
    return low, low[::-1, ::-1]


def f32(array):
    return jnp.asarray(np.asarray(array, np.float32))


def shifted(shard, axis, by):
    count = lax.axis_size(axis)
    return lax.ppermute(shard, axis, [(i, (i + by) % count) for i in range(count)])


def per_device(velocity):
    shape = velocity.shape
    ny, nz = shape[2], shape[3]
    u = velocity.reshape(shape[0] * shape[1], ny, nz)
    lines = u.reshape(-1, nz)
    cells_y, cells_z = np.arange(ny), np.arange(nz)

    up_y = jnp.einsum("kj,pjz->pkz", f32(operator([ny, ny + 1], cells_y)), u, precision=best)
    down_y = jnp.einsum("kj,pjz->pkz", f32(operator([-2, -1], cells_y)), u, precision=best)
    up_z = jnp.einsum("kj,lj->kl", f32(operator([nz, nz + 1], cells_z)), lines, precision=best)
    down_z = jnp.einsum("kj,lj->kl", f32(operator([-2, -1], cells_z)), lines, precision=best)

    low_y = shifted(up_y, "gy", 1)
    high_y = shifted(down_y, "gy", -1)
    low_z = shifted(up_z, "gz", 1)
    high_z = shifted(down_z, "gz", -1)

    local_y = jnp.einsum("ij,pjz->piz", f32(operator(cells_y, cells_y)), u, precision=best)
    local_z = jnp.einsum("lj,ij->li", lines, f32(operator(cells_z, cells_z)), precision=best)

    spread_low_y, spread_high_y = tails(ny)
    spread_low_z, spread_high_z = tails(nz)
    deriv_y = local_y + jnp.einsum("ik,pkz->piz", f32(spread_low_y), low_y, precision=best)
    deriv_y = deriv_y + jnp.einsum("ik,pkz->piz", f32(spread_high_y), high_y, precision=best)
    deriv_z = local_z + jnp.einsum("kl,ik->li", low_z, f32(spread_low_z), precision=best)
    deriv_z = deriv_z + jnp.einsum("kl,ik->li", high_z, f32(spread_high_z), precision=best)
    return deriv_y.reshape(shape), deriv_z.reshape(shape)


def solution(mesh):
    in_specs = (P(None, None, "gy", "gz"),)
    out_specs = (P(None, None, "gy", "gz"), P(None, None, "gy", "gz"))
    return jax.shard_map(
        per_device, mesh=mesh, in_specs=in_specs, out_specs=out_specs, check_vma=False
    )
```

time: 135 us -> 35 us (0.26)
  local copies, waits for them, and re-layouts: 73.8 us -> 2.53 us
  starting transfers between devices: 42.7 us -> 25.8 us
  waiting for transfers between devices: 10.3 us -> 0.01 us
  other arithmetic: 3.31 us -> 0 us
  matrix products: 2.93 us -> 5.19 us
    unnamed x8 -> x22, local copies, waits for them, and re-layouts: 45.5 us -> 1.61 us
    all_to_all x2 -> x0, starting transfers between devices: 23.4 us -> none  [the longest x1 17.5 us: z_regroup(): lax.all_to_all(velocity, 'gz', split_axis=2, concat_axis=3, tiled=True)]
    ppermute x2 -> x4, starting transfers between devices: 5.81 us -> 25.8 us  [shifted(): lax.ppermute(shard, axis, [(i, (i + by) % count) for i in range(count)])]
    all_to_all x5 -> x0, local copies, waits for them, and re-layouts: 17.3 us -> none  [the longest x3 16.9 us: z_regroup(): return lax.all_to_all(result, 'gz', split_axis=3, concat_axis=2, tiled=True)]
    ppermute x2 -> x0, starting transfers between devices: 13.4 us -> none  [the longest x1 11.5 us: padded_2(): lax.ppermute(lax.slice_in_dim(block, 0, width, axis=dim), axis, backward)]
    reshape x1 -> x0, local copies, waits for them, and re-layouts: 9.05 us -> none  [z_regroup(): result = result.reshape(shape_in)]
    ppermute x2 -> x4, waiting for transfers between devices: 8.69 us -> 0.01 us  [shifted(): lax.ppermute(shard, axis, [(i, (i + by) % count) for i in range(count)])]
    dot_general x5 -> x10, matrix products: 2.93 us -> 5.19 us  [the longest x1 1.27 us: per_device(): jnp.einsum('ik,pkz->piz', f32(spread_low_y), low_y, precision=best)]
  transfers between devices with their start and end apart: 6 -> 4, of which waited for: 3 -> 0; matrix products, arithmetic and copies ran while one was open for 26% -> 13% of each run, Pallas kernels for 0% -> 0%
where the time goes in v1:
time: 35 us; the launch traced here: 34.3 us
  starting transfers between devices  25.8 us (74%)
  matrix products  5.19 us (15%)
  local copies, waits for them, and re-layouts  2.53 us (7%)
  between operations  0.8 us (2%)
    ppermute x4, starting transfers between devices, shifted(): lax.ppermute(shard, axis, [(i, (i + by) % count) for i in range(count)])  25.8 us
    unnamed x22, local copies, waits for them, and re-layouts  1.61 us
    dot_general x1, matrix products, per_device(): jnp.einsum('ik,pkz->piz', f32(spread_low_y), low_y, precision=best)  1.27 us
    add x1, local copies, waits for them, and re-layouts, per_device(): deriv_z + jnp.einsum('kl,ik->li', high_z, f32(spread_high_z), precision=b...  0.91 us
  transfers between devices with their start and end apart: 4, of which 0 were waited for; matrix products, arithmetic and copies ran while one was open for 13% of the time, Pallas kernels for 0%

profile of v1, /device:TPU:1, one launch (start us, length us, event | category | flops | bytes accessed | tf_op | source)
XLA Modules:
  0.0 34.3 jit_solution(17934347349861940441)
XLA Ops:
  0.6 0.0 copy-start
  0.6 0.0 copy-start.9
  0.7 1.0 %copy-done = f32[3,2,64,256]{3,2,1,0:T(8,128)S(1)} copy-done((f32[3,2,64,256]{3,2,1,0:T(8,128)S(1)}, f32[3,2,64,256]{3,2,1,0:T(8,128)}, u32[]{:S(2)}) %copy-start) | copy-done | bytes 393240
  1.6 0.0 copy-done.9
  1.6 0.0 copy-start.8
  1.6 0.3 convolution_bitcast_fusion.2
  1.9 21.6 %collective-permute-start.1 = (f32[6,2,256]{2,1,0:T(2,128)S(1)}, f32[6,2,256]{2,1,0:T(2,128)S(1)}, u32[]{:S(2)}, u32[]{:S(2)}) collective-permute-start(f32[6,2,256]{2,1,0:T(2,128)S(1)} %convolution_bitcast_fusion.2), channel_id=1, source_target_pairs={{0,1008},{16,0},{32,16},{48,32},{64,48},{80,64},{96,80},{112,96},{... | collective-permute-start | bytes 36872 | tf_op jit(solution)/shard_map/ppermute | solution.py:45
  23.5 0.0 copy-done.8
  23.5 0.0 copy-start.6
  23.5 0.3 convolution_bitcast_fusion.3
  23.8 1.9 %collective-permute-start = (f32[6,2,256]{2,1,0:T(2,128)S(1)}, f32[6,2,256]{2,1,0:T(2,128)S(1)}, u32[]{:S(2)}, u32[]{:S(2)}) collective-permute-start(f32[6,2,256]{2,1,0:T(2,128)S(1)} %convolution_bitcast_fusion.3), channel_id=1, source_target_pairs={{0,16},{16,32},{32,48},{48,64},{64,80},{80,96},{96,112},{112,128},... | collective-permute-start | bytes 36872 | tf_op jit(solution)/shard_map/ppermute | solution.py:45
  25.8 0.0 copy-done.6
  25.8 0.0 copy-start.5
  25.8 0.4 %fusion.4 = f32[2,384]{1,0:T(2,128)S(1)} fusion(f32[2,256]{1,0:T(2,128)S(1)} %copy-done.6, f32[384,256]{1,0:T(8,128)S(1)} %bitcast.44), kind=kOutput, calls=%fused_computation.10 | convolution fusion | flops 2359296 | bytes 398336 | tf_op jit(solution)/shard_map/kj,lj->kl/dot_general | solution.py:58
  26.2 0.0 copy-start.1
  26.2 1.0 %collective-permute-start.3 = (f32[2,384]{1,0:T(2,128)S(1)}, f32[2,384]{1,0:T(2,128)S(1)}, u32[]{:S(2)}, u32[]{:S(2)}) collective-permute-start(f32[2,384]{1,0:T(2,128)S(1)} %fusion.4), channel_id=1, source_target_pairs={{0,15},{1,0},{2,1},{3,2},{4,3},{5,4},{6,5},{7,6},{8,7},{9,8},{10,9... | collective-permute-start | bytes 9224 | tf_op jit(solution)/shard_map/ppermute | solution.py:45
  27.2 0.0 copy-done.5
  27.2 0.4 %fusion.3 = f32[2,384]{1,0:T(2,128)S(1)} fusion(f32[2,256]{1,0:T(2,128)S(1)} %copy-done.5, f32[384,256]{1,0:T(8,128)S(1)} %bitcast.43), kind=kOutput, calls=%fused_computation.9 | convolution fusion | flops 2359296 | bytes 398336 | tf_op jit(solution)/shard_map/kj,lj->kl/dot_general | solution.py:57
  27.6 0.0 copy-start.4
  27.6 1.3 %collective-permute-start.2 = (f32[2,384]{1,0:T(2,128)S(1)}, f32[2,384]{1,0:T(2,128)S(1)}, u32[]{:S(2)}, u32[]{:S(2)}) collective-permute-start(f32[2,384]{1,0:T(2,128)S(1)} %fusion.3), channel_id=1, source_target_pairs={{0,1},{1,2},{2,3},{3,4},{4,5},{5,6},{6,7},{7,8},{8,9},{9,10},{10,1... | collective-permute-start | bytes 9224 | tf_op jit(solution)/shard_map/ppermute | solution.py:45
  29.0 0.0 copy-done.1
  29.0 0.6 %convolution_bitcast_fusion = f32[384,256]{0,1:T(8,128)S(1)} fusion(f32[256,256]{1,0:T(8,128)S(1)} %copy-done.1, f32[384,256]{1,0:T(8,128)S(1)} %bitcast.42), kind=kOutput, calls=%fused_computation | convolution fusion | flops 301989888 | bytes 1048576 | tf_op jit(solution)/shard_map/lj,ij->li/dot_general | solution.py:66
  29.6 0.0 copy-done.4
  29.6 0.0 copy-start.3
  29.6 0.5 %convolution_bitcast_fusion.1 = f32[6,256,64]{1,2,0:T(8,128)S(1)} fusion(f32[64,64,1]{1,0,2:T(8,128)S(1)} %copy-done.4, f32[6,64,256]{2,1,0:T(8,128)S(1)} %bitcast.39), kind=kOutput, calls=%fused_computation.1 | convolution fusion | flops 75497472 | bytes 802816 | tf_op jit(solution)/shard_map/ij,pjz->piz/dot_general | solution.py:65
  30.1 0.0 copy-start.2
  30.1 0.0 collective-permute-done.3
  30.1 0.4 %copy-done.3 = f32[256,2]{1,0:T(8,128)S(1)} copy-done((f32[256,2]{1,0:T(8,128)S(1)}, f32[256,2]{1,0:T(8,128)}, u32[]{:S(2)}) %copy-start.3) | copy-done | bytes 2072
  30.5 0.4 %fusion.5 = f32[384,256]{0,1:T(8,128)S(1)} fusion(f32[2,384]{1,0:T(2,128)S(1)} %collective-permute-done.3, f32[256,2]{1,0:T(8,128)S(1)} %copy-done.3), kind=kOutput, calls=%fused_computation.11 | convolution fusion | flops 2359296 | bytes 398336 | tf_op jit(solution)/shard_map/kl,ik->li/dot_general | solution.py:73
  30.9 0.0 collective-permute-done.2
  31.0 0.0 copy-done.2
  31.0 0.5 %fusion.1 = f32[384,256]{0,1:T(8,128)S(1)} fusion(f32[384,256]{0,1:T(8,128)S(1)} %fusion.5, f32[384,256]{0,1:T(8,128)S(1)} %convolution_bitcast_fusion, f32[2,384]{1,0:T(2,128)S(1)} %collective-permute-done.2, f32[256,2]{1,0:T(8,128)S(1)} %copy-done.2), kind=kOutput, calls=%fused_computation.5 | convolution fusion | flops 2555904 | bytes 1184768 | tf_op jit(solution)/shard_map/kl,ik->li/dot_general | solution.py:72
  31.5 0.0 copy-start.7
  31.5 0.9 %copy.18 = f32[384,256]{1,0:T(8,128)} copy(f32[384,256]{0,1:T(8,128)S(1)} %fusion.1) | data formatting | bytes 786432 | tf_op jit(solution)/shard_map/add | solution.py:73
  32.4 0.0 copy-start.10
  32.4 0.0 collective-permute-done.1
  32.4 0.0 copy-done.7
  32.4 0.5 %fusion.2 = f32[6,256,64]{1,2,0:T(8,128)S(1)} fusion(f32[6,2,256]{2,1,0:T(2,128)S(1)} %collective-permute-done.1, f32[64,2,1]{0,1,2:T(2,128)S(1)} %copy-done.7), kind=kOutput, calls=%fused_computation.8 | convolution fusion | flops 2359296 | bytes 406016 | tf_op jit(solution)/shard_map/ik,pkz->piz/dot_general | solution.py:71
  32.9 0.0 collective-permute-done
  32.9 0.2 copy-done.10
  33.1 1.3 %fusion = f32[6,256,64]{1,2,0:T(8,128)} fusion(f32[6,256,64]{1,2,0:T(8,128)S(1)} %fusion.2, f32[6,256,64]{1,2,0:T(8,128)S(1)} %convolution_bitcast_fusion.1, f32[6,2,256]{2,1,0:T(2,128)S(1)} %collective-permute-done, f32[64,2,1]{0,1,2:T(2,128)S(1)} %copy-done.10), kind=kOutput, calls=%fused_computation.4 | convolution fusion | flops 2555904 | bytes 1192448 | tf_op jit(solution)/shard_map/ik,pkz->piz/dot_general | solution.py:70
Async XLA Ops:
  0.6 1.0 %copy-start = (f32[3,2,64,256]{3,2,1,0:T(8,128)S(1)}, f32[3,2,64,256]{3,2,1,0:T(8,128)}, u32[]{:S(2)}) copy-start(f32[3,2,64,256]{3,2,1,0:T(8,128)} %param.11) | copy-start | bytes 1179652
  0.6 1.0 %copy-start.9 = (f32[2,64,1]{1,0,2:T(2,128)S(1)}, f32[2,64,1]{1,0,2:T(2,128)}, u32[]{:S(2)}) copy-start(f32[2,64,1]{1,0,2:T(2,128)} %constant.33) | copy-start | bytes 1540
  1.6 21.9 %copy-start.8 = (f32[2,64,1]{1,0,2:T(2,128)S(1)}, f32[2,64,1]{1,0,2:T(2,128)}, u32[]{:S(2)}) copy-start(f32[2,64,1]{1,0,2:T(2,128)} %constant.31) | copy-start | bytes 1540
  1.9 30.4 %collective-permute-start.1 = (f32[6,2,256]{2,1,0:T(2,128)S(1)}, f32[6,2,256]{2,1,0:T(2,128)S(1)}, u32[]{:S(2)}, u32[]{:S(2)}) collective-permute-start(f32[6,2,256]{2,1,0:T(2,128)S(1)} %convolution_bitcast_fusion.2), channel_id=1, source_target_pairs={{0,1008},{16,0},{32,16},{48,32},{64,48},{80,64},{96,80},{112,96},{... | collective-permute-start | bytes 36872 | tf_op jit(solution)/shard_map/ppermute | solution.py:45
  23.5 2.2 %copy-start.6 = (f32[2,256]{1,0:T(2,128)S(1)}, f32[2,256]{1,0:T(2,128)}, u32[]{:S(2)}) copy-start(f32[2,256]{1,0:T(2,128)} %constant.23.clone) | copy-start | bytes 6148
  23.8 9.1 %collective-permute-start = (f32[6,2,256]{2,1,0:T(2,128)S(1)}, f32[6,2,256]{2,1,0:T(2,128)S(1)}, u32[]{:S(2)}, u32[]{:S(2)}) collective-permute-start(f32[6,2,256]{2,1,0:T(2,128)S(1)} %convolution_bitcast_fusion.3), channel_id=1, source_target_pairs={{0,16},{16,32},{32,48},{48,64},{64,80},{80,96},{96,112},{112,128},... | collective-permute-start | bytes 36872 | tf_op jit(solution)/shard_map/ppermute | solution.py:45
  25.8 1.4 %copy-start.5 = (f32[2,256]{1,0:T(2,128)S(1)}, f32[2,256]{1,0:T(2,128)}, u32[]{:S(2)}) copy-start(f32[2,256]{1,0:T(2,128)} %constant.22.clone) | copy-start | bytes 6148
  26.2 2.8 %copy-start.1 = (f32[256,256]{1,0:T(8,128)S(1)}, f32[256,256]{1,0:T(8,128)}, u32[]{:S(2)}) copy-start(f32[256,256]{1,0:T(8,128)} %constant.25.clone) | copy-start | bytes 786436
  26.2 3.9 %collective-permute-start.3 = (f32[2,384]{1,0:T(2,128)S(1)}, f32[2,384]{1,0:T(2,128)S(1)}, u32[]{:S(2)}, u32[]{:S(2)}) collective-permute-start(f32[2,384]{1,0:T(2,128)S(1)} %fusion.4), channel_id=1, source_target_pairs={{0,15},{1,0},{2,1},{3,2},{4,3},{5,4},{6,5},{7,6},{8,7},{9,8},{10,9... | collective-permute-start | bytes 9224 | tf_op jit(solution)/shard_map/ppermute | solution.py:45
  27.6 1.9 %copy-start.4 = (f32[64,64,1]{1,0,2:T(8,128)S(1)}, f32[64,64,1]{1,0,2:T(8,128)}, u32[]{:S(2)}) copy-start(f32[64,64,1]{1,0,2:T(8,128)} %constant.30) | copy-start | bytes 49156
  27.6 3.3 %collective-permute-start.2 = (f32[2,384]{1,0:T(2,128)S(1)}, f32[2,384]{1,0:T(2,128)S(1)}, u32[]{:S(2)}, u32[]{:S(2)}) collective-permute-start(f32[2,384]{1,0:T(2,128)S(1)} %fusion.3), channel_id=1, source_target_pairs={{0,1},{1,2},{2,3},{3,4},{4,5},{5,6},{6,7},{7,8},{8,9},{9,10},{10,1... | collective-permute-start | bytes 9224 | tf_op jit(solution)/shard_map/ppermute | solution.py:45
  29.6 0.9 %copy-start.3 = (f32[256,2]{1,0:T(8,128)S(1)}, f32[256,2]{1,0:T(8,128)}, u32[]{:S(2)}) copy-start(f32[256,2]{1,0:T(8,128)} %constant.29.clone) | copy-start | bytes 6148
  30.1 0.9 %copy-start.2 = (f32[256,2]{1,0:T(8,128)S(1)}, f32[256,2]{1,0:T(8,128)}, u32[]{:S(2)}) copy-start(f32[256,2]{1,0:T(8,128)} %constant.28.clone) | copy-start | bytes 6148
  31.5 0.9 %copy-start.7 = (f32[64,2,1]{0,1,2:T(2,128)S(1)}, f32[64,2,1]{0,1,2:T(2,128)}, u32[]{:S(2)}) copy-start(f32[64,2,1]{0,1,2:T(2,128)} %constant.34) | copy-start | bytes 1540
  32.4 0.7 %copy-start.10 = (f32[64,2,1]{0,1,2:T(2,128)S(1)}, f32[64,2,1]{0,1,2:T(2,128)}, u32[]{:S(2)}) copy-start(f32[64,2,1]{0,1,2:T(2,128)} %constant.32) | copy-start | bytes 1540

commit v2 on v1

v2 whole, which is shorter than its diff:
```python
import math

import jax
import jax.numpy as jnp
import numpy as np
from jax import lax
from jax.experimental import pallas as pl
from jax.experimental.pallas import tpu as pltpu
from jax.sharding import PartitionSpec as P

best = lax.Precision.HIGHEST
vmem = 4 << 20
root = 1.5 - math.sqrt(5.0) / 2.0
log_root = math.log2(root)


def response(n):
    scale = root * 3.0 / (1.0 - root * root)

    def green(n):
        return scale * (-1.0) ** abs(n) * root ** abs(n)

    return 7.0 / 9.0 * (green(n + 1) - green(n - 1)) + 1.0 / 36.0 * (green(n + 2) - green(n - 2))


far_scale = response(2) / root**2
near_extra = response(1) + far_scale * root


def decay(n):
    return jnp.where(n % 2 == 0, 1.0, -1.0) * jnp.exp2(n.astype(jnp.float32) * log_root)


def operator(shape, row_start, row_dim):
    lag = row_start + lax.broadcasted_iota(jnp.int32, shape, row_dim) - lax.broadcasted_iota(jnp.int32, shape, 1 - row_dim)
    size = jnp.abs(lag)
    weight = far_scale * decay(size) + jnp.where(size == 1, near_extra, 0.0)
    return jnp.where(lag == 0, 0.0, jnp.where(lag > 0, weight, -weight))


def edges_kernel(u_hbm, up_ref, down_ref, u_ref, sem):
    planes, ny, nz = u_ref.shape
    copies = [pltpu.make_async_copy(u_hbm.at[p], u_ref.at[p], sem.at[p]) for p in range(planes)]
    for copy in copies:
        copy.start()
    row = lax.broadcasted_iota(jnp.int32, (ny, nz), 0)
    up_weight = far_scale * decay(ny + 1 - row)
    down_weight = -far_scale * decay(row + 2)
    for p in range(planes):
        copies[p].wait()
        u = u_ref[p]
        up = jnp.sum(u * up_weight, axis=0, keepdims=True)
        down = jnp.sum(u * down_weight, axis=0, keepdims=True)
        up_ref[p, 0:1, :] = up * (-1.0 / root) + near_extra * u[ny - 1 : ny]
        up_ref[p, 1:2, :] = up
        down_ref[p, 0:1, :] = down
        down_ref[p, 1:2, :] = down * (-1.0 / root) - near_extra * u[0:1]


def edges(u):
    planes, ny, nz = u.shape
    out = jax.ShapeDtypeStruct((planes, 2, nz), jnp.float32)
    return pl.pallas_call(
        edges_kernel,
        out_shape=(out, out),
        in_specs=[pl.BlockSpec(memory_space=pl.ANY)],
        out_specs=(pl.BlockSpec(memory_space=pltpu.VMEM), pl.BlockSpec(memory_space=pltpu.VMEM)),
        scratch_shapes=[pltpu.VMEM(u.shape, jnp.float32), pltpu.SemaphoreType.DMA((planes,))],
        compiler_params=pltpu.CompilerParams(vmem_limit_bytes=vmem),
        name="edges_y",
    )(u)


def join_kernel(local_ref, low_ref, high_ref, out_hbm, out_ref, sem):
    planes, ny, nz = local_ref.shape
    row = lax.broadcasted_iota(jnp.int32, (ny, nz), 0)
    low_decay = decay(jnp.maximum(row - 1, 0))
    high_decay = decay(jnp.maximum(ny - 2 - row, 0))
    copies = []
    for p in range(planes):
        low = jnp.where(row == 0, low_ref[p, 0:1, :], low_ref[p, 1:2, :] * low_decay)
        high = jnp.where(row == ny - 1, high_ref[p, 1:2, :], high_ref[p, 0:1, :] * high_decay)
        out_ref[p] = local_ref[p] + low + high
        copies.append(pltpu.make_async_copy(out_ref.at[p], out_hbm.at[p], sem.at[p]))
        copies[p].start()
    for copy in copies:
        copy.wait()


def join(local, low, high):
    planes = local.shape[0]
    return pl.pallas_call(
        join_kernel,
        out_shape=jax.ShapeDtypeStruct(local.shape, jnp.float32),
        in_specs=[pl.BlockSpec(memory_space=pltpu.VMEM)] * 3,
        out_specs=pl.BlockSpec(memory_space=pl.ANY),
        scratch_shapes=[pltpu.VMEM(local.shape, jnp.float32), pltpu.SemaphoreType.DMA((planes,))],
        compiler_params=pltpu.CompilerParams(vmem_limit_bytes=vmem),
        name="join_y",
    )(local, low, high)


def local_kernel(u_ref, z_ref, y_ref):
    planes, ny, nz = u_ref.shape
    along = operator((nz, nz), 0, 1)
    across = operator((ny, ny), 0, 0)
    for p in range(planes):
        z_ref[p] = jnp.dot(u_ref[p], along, precision=best, preferred_element_type=jnp.float32)
        y_ref[p] = jnp.dot(across, u_ref[p], precision=best, preferred_element_type=jnp.float32)


def local_parts(u):
    out = jax.ShapeDtypeStruct(u.shape, jnp.float32)
    here = pl.BlockSpec(memory_space=pltpu.VMEM)
    return pl.pallas_call(
        local_kernel,
        out_shape=(out, out),
        in_specs=[here],
        out_specs=(here, here),
        compiler_params=pltpu.CompilerParams(vmem_limit_bytes=vmem),
        cost_estimate=pl.CostEstimate(flops=2 * u.size * 512, bytes_accessed=12 * u.size, transcendentals=70000),
        name="local_parts",
    )(u)


def join_z_kernel(local_ref, low_ref, high_ref, out_hbm, out_ref, sem):
    planes, ny, nz = local_ref.shape
    ends = jnp.concatenate([low_ref[...], high_ref[...], low_ref[...], high_ref[...]], axis=0)
    ends = jnp.transpose(ends)
    cell = lax.broadcasted_iota(jnp.int32, (1, nz), 1)
    low_first = jnp.where(cell == 0, 1.0, 0.0)
    low_rest = jnp.where(cell == 0, 0.0, decay(jnp.maximum(cell - 1, 0)))
    high_first = jnp.where(cell == nz - 1, 1.0, 0.0)
    high_rest = jnp.where(cell == nz - 1, 0.0, decay(jnp.maximum(nz - 2 - cell, 0)))
    copies = []
    for p in range(planes):
        end = ends[p * ny : (p + 1) * ny]
        low = end[:, 0:1] * low_first + end[:, 1:2] * low_rest
        high = end[:, 2:3] * high_rest + end[:, 3:4] * high_first
        out_ref[p] = local_ref[p] + low + high
        copies.append(pltpu.make_async_copy(out_ref.at[p], out_hbm.at[p], sem.at[p]))
        copies[p].start()
    for copy in copies:
        copy.wait()


def join_z(local, low, high):
    planes = local.shape[0]
    return pl.pallas_call(
        join_z_kernel,
        out_shape=jax.ShapeDtypeStruct(local.shape, jnp.float32),
        in_specs=[pl.BlockSpec(memory_space=pltpu.VMEM)] * 3,
        out_specs=pl.BlockSpec(memory_space=pl.ANY),
        scratch_shapes=[pltpu.VMEM(local.shape, jnp.float32), pltpu.SemaphoreType.DMA((planes,))],
        compiler_params=pltpu.CompilerParams(vmem_limit_bytes=vmem),
        name="join_z",
    )(local, low, high)


def place_kernel(u_hbm, out_hbm):
    pass


def place(u):
    return pl.pallas_call(
        place_kernel,
        out_shape=jax.ShapeDtypeStruct(u.shape, u.dtype),
        in_specs=[pl.BlockSpec(memory_space=pl.ANY)],
        out_specs=pl.BlockSpec(memory_space=pl.ANY),
        compiler_params=pltpu.CompilerParams(vmem_limit_bytes=vmem),
        name="place_z",
    )(u)


def shifted(shard, axis, by):
    count = lax.axis_size(axis)
    return lax.ppermute(shard, axis, [(i, (i + by) % count) for i in range(count)])


def along_z(u):
    nz = u.shape[2]
    lines = u.reshape(-1, nz)
    up = jnp.einsum("kj,lj->kl", operator((2, nz), nz, 0), lines, precision=best)
    down = jnp.einsum("kj,lj->kl", operator((2, nz), -2, 0), lines, precision=best)
    low = shifted(up, "gz", 1)
    high = shifted(down, "gz", -1)
    local_z, local_y = local_parts(u)
    return join_z(local_z, low, high), local_y


def per_device(velocity):
    shape = velocity.shape
    u = velocity.reshape(shape[0] * shape[1], shape[2], shape[3])
    late = lax.axis_index("gy") % 8 == 7
    up_y, down_y = edges(u)
    low_y = shifted(up_y, "gy", 1)
    deriv_z, local_y = lax.cond(
        late, lambda u: (place(u), jnp.zeros_like(u)), along_z, u
    )
    down_y, deriv_z, local_y = lax.optimization_barrier((down_y, deriv_z, local_y))
    high_y = shifted(down_y, "gy", -1)
    deriv_z, local_y = lax.cond(late, lambda u, z, y: along_z(u), lambda u, z, y: (z, y), u, deriv_z, local_y)
    deriv_y = join(local_y, low_y, high_y)
    return deriv_y.reshape(shape), deriv_z.reshape(shape)


def solution(mesh):
    in_specs = (P(None, None, "gy", "gz"),)
    out_specs = (P(None, None, "gy", "gz"), P(None, None, "gy", "gz"))
    return jax.shard_map(
        per_device, mesh=mesh, in_specs=in_specs, out_specs=out_specs, check_vma=False
    )
```

time: 35 us -> 29 us (0.83)
  the two profiles are of different devices: /device:TPU:1 before, /device:TPU:15 now
where the time goes in v2:
time: 29 us; the launch traced here: 28.8 us
  starting transfers between devices  17.2 us (59%)
  waiting for transfers between devices  5.37 us (19%)
  Pallas kernels  4.63 us (16%)
  matrix products  0.82 us (3%)
  between operations  0.72 us (2%)
    ppermute x4, starting transfers between devices, shifted(): lax.ppermute(shard, axis, [(i, (i + by) % count) for i in range(count)])  17.2 us
    ppermute x4, waiting for transfers between devices, shifted(): lax.ppermute(shard, axis, [(i, (i + by) % count) for i in range(count)])  5.37 us
    pallas_call x1, Pallas kernels, local_parts(): pl.pallas_call(local_kernel, out_shape=(out, out), in_specs=[here], out_s...  1.38 us
    pallas_call x1, Pallas kernels, join_z(): pl.pallas_call(join_z_kernel, out_shape=jax.ShapeDtypeStruct(local.shape,...  1.3 us
    pallas_call x1, Pallas kernels, edges(): pl.pallas_call(edges_kernel, out_shape=(out, out), in_specs=[pl.BlockSpec...  1.12 us
    pallas_call x1, Pallas kernels, join(): pl.pallas_call(join_kernel, out_shape=jax.ShapeDtypeStruct(local.shape, j...  0.83 us
  transfers between devices with their start and end apart: 4, of which 2 were waited for; matrix products, arithmetic and copies ran while one was open for 3% of the time, Pallas kernels for 9%

profile of v2, /device:TPU:15, one launch (start us, length us, event | category | flops | bytes accessed | tf_op | source)
XLA Modules:
  0.0 28.8 jit_solution(11906522842460093169)
XLA Ops:
  0.6 0.0 copy-start
  0.6 1.1 %edges_y.1 = (f32[6,2,256]{2,1,0:T(2,128)S(1)}, f32[6,2,256]{2,1,0:T(2,128)S(1)}) custom-call(f32[6,64,256]{2,1,0:T(8,128)} %bitcast.10), custom_call_target="tpu_custom_call" | custom-call | tf_op jit(solution)/shard_map/edges_y/pallas_call | solution.py:63
  1.8 4.9 %collective-permute-start.4 = (f32[6,2,256]{2,1,0:T(2,128)S(1)}, f32[6,2,256]{2,1,0:T(2,128)S(1)}, u32[]{:S(2)}, u32[]{:S(2)}) collective-permute-start(f32[6,2,256]{2,1,0:T(2,128)S(1)} %get-tuple-element.43), channel_id=1, source_target_pairs={{0,16},{16,32},{32,48},{48,64},{64,80},{80,96},{96,112},{112,128},... | collective-permute-start | bytes 36872 | tf_op jit(solution)/shard_map/ppermute | solution.py:177
  6.7 0.0 copy-done
  6.7 16.8 %conditional.2 = (f32[6,64,256]{2,1,0:T(8,128)S(1)}, f32[6,64,256]{2,1,0:T(8,128)S(1)}) conditional(s32[]{:T(128)} %convert_element_type.16, (f32[6,64,256]{2,1,0:T(8,128)S(1)}, f32[3,2,64,256]{3,2,1,0:T(8,128)S(1)}) %tuple.41, f32[6,64,256]{2,1,0:T(8,128)S(1)} %bitcast.11), branch_computations={%region_0.1_spmd, %region_1.2_spmd} | conditional | flops 105409536 | bytes 1996928 | solution.py:197
  6.7 0.4 %fusion = f32[2,384]{1,0:T(2,128)S(1)} fusion(f32[384,256]{1,0:T(8,128)S(1)} %bitcast.14, s32[2]{0:T(128)S(1)} %iota_add_fusion.1), kind=kOutput, calls=%fused_computation.14 | convolution fusion | flops 2373120 | bytes 396296 | tf_op jit(solution)/shard_map/cond/branch_0_fun/kj,lj->kl/dot_general | solution.py:183
  7.1 10.4 %collective-permute-start = (f32[2,384]{1,0:T(2,128)S(1)}, f32[2,384]{1,0:T(2,128)S(1)}, u32[]{:S(2)}, u32[]{:S(2)}) collective-permute-start(f32[2,384]{1,0:T(2,128)S(1)} %fusion), channel_id=1, source_target_pairs={{0,1},{1,2},{2,3},{3,4},{4,5},{5,6},{6,7},{7,8},{8,9},{9,10},{10,1... | collective-permute-start | bytes 9224 | tf_op jit(solution)/shard_map/cond/branch_0_fun/ppermute | solution.py:177
  17.5 0.4 %fusion.4 = f32[2,384]{1,0:T(2,128)S(1)} fusion(f32[384,256]{1,0:T(8,128)S(1)} %bitcast.15, s32[2]{0:T(128)S(1)} %iota_add_fusion), kind=kOutput, calls=%fused_computation.17 | convolution fusion | flops 2373120 | bytes 396296 | tf_op jit(solution)/shard_map/cond/branch_0_fun/kj,lj->kl/dot_general | solution.py:184
  17.9 0.0 collective-permute-start.1
  17.9 1.4 %local_parts.2 = (f32[6,64,256]{2,1,0:T(8,128)S(1)}, f32[6,64,256]{2,1,0:T(8,128)S(1)}) custom-call(f32[6,64,256]{2,1,0:T(8,128)S(1)} %bitcast.16), custom_call_target="tpu_custom_call" | custom-call | flops 100663296 | bytes 1179648 | tf_op jit(solution)/shard_map/cond/branch_0_fun/local_parts/pallas_call | solution.py:115
  19.3 0.0 collective-permute-done.low_ref
  19.3 2.9 %collective-permute-done.1.high_ref = f32[2,384]{1,0:T(2,128)S(1)} collective-permute-done((f32[2,384]{1,0:T(2,128)S(1)}, f32[2,384]{1,0:T(2,128)S(1)}, u32[]{:S(2)}, u32[]{:S(2)}) %collective-permute-start.1) | collective-permute-done | bytes 3104 | tf_op jit(solution)/shard_map/cond/branch_0_fun/ppermute | solution.py:177
  22.2 1.3 %join_z.2 = f32[6,64,256]{2,1,0:T(8,128)S(1)} custom-call(f32[6,64,256]{2,1,0:T(8,128)S(1)} %get-tuple-element.19.local_ref, f32[2,384]{1,0:T(2,128)S(1)} %collective-permute-done.low_ref, f32[2,384]{1,0:T(2,128)S(1)} %collective-permute-done.1.high_ref), custom_call_target="tpu_custom_call" | custom-call | tf_op jit(solution)/shard_map/cond/branch_0_fun/join_z/pallas_call | solution.py:149
  23.6 1.9 %collective-permute-start.5 = (f32[6,2,256]{2,1,0:T(2,128)S(1)}, f32[6,2,256]{2,1,0:T(2,128)S(1)}, u32[]{:S(2)}, u32[]{:S(2)}) collective-permute-start(f32[6,2,256]{2,1,0:T(2,128)S(1)} %get-tuple-element.44), channel_id=1, source_target_pairs={{0,1008},{16,0},{32,16},{48,32},{64,48},{80,64},{96,80},{112,96},{... | collective-permute-start | bytes 36872 | tf_op jit(solution)/shard_map/ppermute | solution.py:177
  25.5 0.0 copy-start.1
  25.5 0.0 collective-permute-done.4.low_ref
  25.5 2.5 %collective-permute-done.5.high_ref = f32[6,2,256]{2,1,0:T(2,128)S(1)} collective-permute-done((f32[6,2,256]{2,1,0:T(2,128)S(1)}, f32[6,2,256]{2,1,0:T(2,128)S(1)}, u32[]{:S(2)}, u32[]{:S(2)}) %collective-permute-start.5) | collective-permute-done | bytes 12320 | tf_op jit(solution)/shard_map/ppermute | solution.py:177
  28.0 0.8 %join_y.1 = f32[6,64,256]{2,1,0:T(8,128)} custom-call(f32[6,64,256]{2,1,0:T(8,128)S(1)} %get-tuple-element.42.local_ref, f32[6,2,256]{2,1,0:T(2,128)S(1)} %collective-permute-done.4.low_ref, f32[6,2,256]{2,1,0:T(2,128)S(1)} %collective-permute-done.5.high_ref), custom_call_target="tpu_custom_call" | custom-call | tf_op jit(solution)/shard_map/join_y/pallas_call | solution.py:92
  28.8 0.0 copy-done.1
  (3 shorter events, 0.0 us)
Async XLA Ops:
  0.6 6.1 %copy-start = (f32[3,2,64,256]{3,2,1,0:T(8,128)S(1)}, f32[3,2,64,256]{3,2,1,0:T(8,128)}, u32[]{:S(2)}) copy-start(f32[3,2,64,256]{3,2,1,0:T(8,128)} %param.5) | copy-start | bytes 1179652
  1.8 23.7 %collective-permute-start.4 = (f32[6,2,256]{2,1,0:T(2,128)S(1)}, f32[6,2,256]{2,1,0:T(2,128)S(1)}, u32[]{:S(2)}, u32[]{:S(2)}) collective-permute-start(f32[6,2,256]{2,1,0:T(2,128)S(1)} %get-tuple-element.43), channel_id=1, source_target_pairs={{0,16},{16,32},{32,48},{48,64},{64,80},{80,96},{96,112},{112,128},... | collective-permute-start | bytes 36872 | tf_op jit(solution)/shard_map/ppermute | solution.py:177
  7.1 12.2 %collective-permute-start = (f32[2,384]{1,0:T(2,128)S(1)}, f32[2,384]{1,0:T(2,128)S(1)}, u32[]{:S(2)}, u32[]{:S(2)}) collective-permute-start(f32[2,384]{1,0:T(2,128)S(1)} %fusion), channel_id=1, source_target_pairs={{0,1},{1,2},{2,3},{3,4},{4,5},{5,6},{6,7},{7,8},{8,9},{9,10},{10,1... | collective-permute-start | bytes 9224 | tf_op jit(solution)/shard_map/cond/branch_0_fun/ppermute | solution.py:177
  17.9 4.3 %collective-permute-start.1 = (f32[2,384]{1,0:T(2,128)S(1)}, f32[2,384]{1,0:T(2,128)S(1)}, u32[]{:S(2)}, u32[]{:S(2)}) collective-permute-start(f32[2,384]{1,0:T(2,128)S(1)} %fusion.4), channel_id=1, source_target_pairs={{0,15},{1,0},{2,1},{3,2},{4,3},{5,4},{6,5},{7,6},{8,7},{9,8},{10,9... | collective-permute-start | bytes 9224 | tf_op jit(solution)/shard_map/cond/branch_0_fun/ppermute | solution.py:177
  23.6 4.4 %collective-permute-start.5 = (f32[6,2,256]{2,1,0:T(2,128)S(1)}, f32[6,2,256]{2,1,0:T(2,128)S(1)}, u32[]{:S(2)}, u32[]{:S(2)}) collective-permute-start(f32[6,2,256]{2,1,0:T(2,128)S(1)} %get-tuple-element.44), channel_id=1, source_target_pairs={{0,1008},{16,0},{32,16},{48,32},{64,48},{80,64},{96,80},{112,96},{... | collective-permute-start | bytes 36872 | tf_op jit(solution)/shard_map/ppermute | solution.py:177
  25.5 3.3 %copy-start.1 = (f32[3,2,64,256]{3,2,1,0:T(8,128)}, f32[3,2,64,256]{3,2,1,0:T(8,128)S(1)}, u32[]{:S(2)}) copy-start(f32[3,2,64,256]{3,2,1,0:T(8,128)S(1)} %get-tuple-element.36) | copy-start | bytes 1179652

commit v3 on v2

--- a/solution.py
+++ b/solution.py
@@ -10,6 +10,7 @@
 
 best = lax.Precision.HIGHEST
 vmem = 4 << 20
+column = 8
 root = 1.5 - math.sqrt(5.0) / 2.0
 log_root = math.log2(root)
 
@@ -38,8 +39,9 @@
     return jnp.where(lag == 0, 0.0, jnp.where(lag > 0, weight, -weight))
 
 
-def edges_kernel(u_hbm, up_ref, down_ref, u_ref, sem):
+def edges_kernel(u_hbm, up_ref, down_ref, up_in_ref, down_in_ref, pair_ref, u_ref, sem):
     planes, ny, nz = u_ref.shape
+    even = lax.axis_index("gy") % 2 == 0
     copies = [pltpu.make_async_copy(u_hbm.at[p], u_ref.at[p], sem.at[p]) for p in range(planes)]
     for copy in copies:
         copy.start()
@@ -51,35 +53,42 @@
         u = u_ref[p]
         up = jnp.sum(u * up_weight, axis=0, keepdims=True)
         down = jnp.sum(u * down_weight, axis=0, keepdims=True)
-        up_ref[p, 0:1, :] = up * (-1.0 / root) + near_extra * u[ny - 1 : ny]
-        up_ref[p, 1:2, :] = up
-        down_ref[p, 0:1, :] = down
-        down_ref[p, 1:2, :] = down * (-1.0 / root) - near_extra * u[0:1]
+        up_near = up * (-1.0 / root) + near_extra * u[ny - 1 : ny]
+        down_near = down * (-1.0 / root) - near_extra * u[0:1]
+        for ref in (up_ref, up_in_ref):
+            ref[p, 0:1, :] = up_near
+            ref[p, 1:2, :] = up
+        for ref in (down_ref, down_in_ref):
+            ref[p, 0:1, :] = down
+            ref[p, 1:2, :] = down_near
+        pair_ref[p, 0:1, :] = jnp.where(even, up_near, down)
+        pair_ref[p, 1:2, :] = jnp.where(even, up, down_near)
 
 
 def edges(u):
     planes, ny, nz = u.shape
-    out = jax.ShapeDtypeStruct((planes, 2, nz), jnp.float32)
+    out = pltpu.VMEM((planes, 2, nz), jnp.float32)
     return pl.pallas_call(
         edges_kernel,
-        out_shape=(out, out),
+        out_shape=(out,) * 5,
         in_specs=[pl.BlockSpec(memory_space=pl.ANY)],
-        out_specs=(pl.BlockSpec(memory_space=pltpu.VMEM), pl.BlockSpec(memory_space=pltpu.VMEM)),
+        out_specs=(pl.BlockSpec(memory_space=pltpu.VMEM),) * 5,
         scratch_shapes=[pltpu.VMEM(u.shape, jnp.float32), pltpu.SemaphoreType.DMA((planes,))],
         compiler_params=pltpu.CompilerParams(vmem_limit_bytes=vmem),
         name="edges_y",
     )(u)
 
 
-def join_kernel(local_ref, low_ref, high_ref, out_hbm, out_ref, sem):
+def join_rows(local_ref, low_of, high_of, out_hbm, out_ref, sem):
     planes, ny, nz = local_ref.shape
     row = lax.broadcasted_iota(jnp.int32, (ny, nz), 0)
     low_decay = decay(jnp.maximum(row - 1, 0))
     high_decay = decay(jnp.maximum(ny - 2 - row, 0))
     copies = []
     for p in range(planes):
-        low = jnp.where(row == 0, low_ref[p, 0:1, :], low_ref[p, 1:2, :] * low_decay)
-        high = jnp.where(row == ny - 1, high_ref[p, 1:2, :], high_ref[p, 0:1, :] * high_decay)
+        low, high = low_of(p), high_of(p)
+        low = jnp.where(row == 0, low[0:1], low[1:2] * low_decay)
+        high = jnp.where(row == ny - 1, high[1:2], high[0:1] * high_decay)
         out_ref[p] = local_ref[p] + low + high
         copies.append(pltpu.make_async_copy(out_ref.at[p], out_hbm.at[p], sem.at[p]))
         copies[p].start()
@@ -87,17 +96,78 @@
         copy.wait()
 
 
-def join(local, low, high):
+def join_kernel(local_ref, wrap_ref, low_ref, high_ref, out_hbm, out_ref, sem):
+    place = lax.axis_index("gy") % column
+
+    @pl.when(place != column - 1)
+    def _():
+        def low(p):
+            return jnp.where(place == 0, wrap_ref[p], low_ref[p])
+
+        join_rows(local_ref, low, lambda p: high_ref[p], out_hbm, out_ref, sem)
+
+
+def join_last_kernel(made_hbm, local_ref, low_ref, wrap_ref, out_hbm, out_ref, sem):
+    @pl.when(lax.axis_index("gy") % column == column - 1)
+    def _():
+        join_rows(local_ref, lambda p: low_ref[p], lambda p: wrap_ref[p], out_hbm, out_ref, sem)
+
+
+def join(local, *ends):
     planes = local.shape[0]
     return pl.pallas_call(
         join_kernel,
         out_shape=jax.ShapeDtypeStruct(local.shape, jnp.float32),
-        in_specs=[pl.BlockSpec(memory_space=pltpu.VMEM)] * 3,
+        in_specs=[pl.BlockSpec(memory_space=pltpu.VMEM)] * 4,
         out_specs=pl.BlockSpec(memory_space=pl.ANY),
         scratch_shapes=[pltpu.VMEM(local.shape, jnp.float32), pltpu.SemaphoreType.DMA((planes,))],
         compiler_params=pltpu.CompilerParams(vmem_limit_bytes=vmem),
+        cost_estimate=pl.CostEstimate(flops=6 * local.size, bytes_accessed=8 * local.size, transcendentals=32768),
         name="join_y",
-    )(local, low, high)
+    )(*(pltpu.with_memory_space_constraint(end, pltpu.VMEM) for end in (local, *ends)))
+
+
+def join_last(made, local, low, wrap):
+    planes = local.shape[0]
+    return pl.pallas_call(
+        join_last_kernel,
+        out_shape=jax.ShapeDtypeStruct(local.shape, jnp.float32),
+        in_specs=[pl.BlockSpec(memory_space=pl.ANY)] + [pl.BlockSpec(memory_space=pltpu.VMEM)] * 3,
+        out_specs=pl.BlockSpec(memory_space=pl.ANY),
+        scratch_shapes=[pltpu.VMEM(local.shape, jnp.float32), pltpu.SemaphoreType.DMA((planes,))],
+        compiler_params=pltpu.CompilerParams(vmem_limit_bytes=vmem),
+        input_output_aliases={0: 0},
+        name="join_y_last",
+    )(made, *(pltpu.with_memory_space_constraint(end, pltpu.VMEM) for end in (local, low, wrap)))
+
+
+def edges_z_kernel(u_ref, up_ref, down_ref):
+    planes, ny, nz = u_ref.shape
+    which = lax.broadcasted_iota(jnp.int32, (8, nz), 0)
+    cell = lax.broadcasted_iota(jnp.int32, (8, nz), 1)
+    target = jnp.where(which < 2, nz + which, which - 4)
+    lag = target - cell
+    size = jnp.abs(lag)
+    weight = far_scale * decay(size) + jnp.where(size == 1, near_extra, 0.0)
+    weight = jnp.where(lag > 0, weight, -weight)
+    ends = lax.dot_general(
+        weight, u_ref[...].reshape(planes * ny, nz), (((1,), (1,)), ((), ())), precision=best, preferred_element_type=jnp.float32
+    )
+    up_ref[...] = ends[0:2]
+    down_ref[...] = ends[2:4]
+
+
+def edges_z(u):
+    out = jax.ShapeDtypeStruct((2, u.shape[0] * u.shape[1]), jnp.float32)
+    here = pl.BlockSpec(memory_space=pltpu.VMEM)
+    return pl.pallas_call(
+        edges_z_kernel,
+        out_shape=(out, out),
+        in_specs=[here],
+        out_specs=(here, here),
+        compiler_params=pltpu.CompilerParams(vmem_limit_bytes=vmem),
+        name="edges_z",
+    )(u)
 
 
 def local_kernel(u_ref, z_ref, y_ref):
@@ -123,7 +193,7 @@
     )(u)
 
 
-def join_z_kernel(local_ref, low_ref, high_ref, out_hbm, out_ref, sem):
+def join_z_kernel(local_ref, high_ref, low_ref, out_hbm, out_ref, sem):
     planes, ny, nz = local_ref.shape
     ends = jnp.concatenate([low_ref[...], high_ref[...], low_ref[...], high_ref[...]], axis=0)
     ends = jnp.transpose(ends)
@@ -154,14 +224,14 @@
         scratch_shapes=[pltpu.VMEM(local.shape, jnp.float32), pltpu.SemaphoreType.DMA((planes,))],
         compiler_params=pltpu.CompilerParams(vmem_limit_bytes=vmem),
         name="join_z",
-    )(local, low, high)
+    )(local, high, low)
 
 
 def place_kernel(u_hbm, out_hbm):
     pass
 
 
-def place(u):
+def place_z(u):
     return pl.pallas_call(
         place_kernel,
         out_shape=jax.ShapeDtypeStruct(u.shape, u.dtype),
@@ -177,30 +247,61 @@
     return lax.ppermute(shard, axis, [(i, (i + by) % count) for i in range(count)])
 
 
-def along_z(u):
-    nz = u.shape[2]
-    lines = u.reshape(-1, nz)
-    up = jnp.einsum("kj,lj->kl", operator((2, nz), nz, 0), lines, precision=best)
-    down = jnp.einsum("kj,lj->kl", operator((2, nz), -2, 0), lines, precision=best)
+def linked(shard, pairs):
+    return lax.ppermute(shard, "gy", pairs)
+
+
+def along_z(u, pair=None, links=None):
+    up, down = edges_z(u)
+    high = shifted(down, "gz", -1)
     low = shifted(up, "gz", 1)
-    high = shifted(down, "gz", -1)
     local_z, local_y = local_parts(u)
-    return join_z(local_z, low, high), local_y
+    if links is None:
+        return join_z(local_z, low, high), local_y
+    high, low, pair = lax.optimization_barrier((high, low, pair))
+    there = lax.ppermute(pair, ("gy", "gz"), links)
+    return join_z(local_z, low, high), local_y, there
 
 
 def per_device(velocity):
     shape = velocity.shape
     u = velocity.reshape(shape[0] * shape[1], shape[2], shape[3])
-    late = lax.axis_index("gy") % 8 == 7
-    up_y, down_y = edges(u)
-    low_y = shifted(up_y, "gy", 1)
-    deriv_z, local_y = lax.cond(
-        late, lambda u: (place(u), jnp.zeros_like(u)), along_z, u
-    )
-    down_y, deriv_z, local_y = lax.optimization_barrier((down_y, deriv_z, local_y))
-    high_y = shifted(down_y, "gy", -1)
-    deriv_z, local_y = lax.cond(late, lambda u, z, y: along_z(u), lambda u, z, y: (z, y), u, deriv_z, local_y)
-    deriv_y = join(local_y, low_y, high_y)
+    count, width = lax.axis_size("gy"), lax.axis_size("gz")
+    row, place = lax.axis_index("gy"), lax.axis_index("gy") % column
+    slow = (lax.axis_index("gz") == 0) & (row < 2)
+    ends = range(count)
+    final = [(i, i ^ 1) for i in ends if i % column >= column - 2]
+    inner = [(i, i + 1) for i in ends if 1 <= i % column < column - 2]
+    wrap = [(i, (i + 1) % count) for i in ends if i % column == column - 1]
+    last = [(0, width), (width, 0)]
+    first = [(i * width + k, (i ^ 1) * width + k) for i in ends if i % column < 2 for k in range(width)]
+    first = [link for link in first if link not in last]
+
+    def back(pairs):
+        return [(b, a) for a, b in pairs]
+
+    def early(u, up, down, pair):
+        pair_in = lax.ppermute(pair, ("gy", "gz"), first)
+        low = linked(up, inner)
+        high = linked(down, back(inner))
+        u, pair_in = lax.optimization_barrier((u, pair_in))
+        deriv_z, local_y, there = along_z(u, pair, last)
+        pair_in = jnp.where(slow, there, pair_in)
+        return deriv_z, local_y, jnp.where(place == 1, pair_in, low), jnp.where(place == 0, pair_in, high)
+
+    def skip(u, up, down, pair):
+        return place_z(u), jnp.zeros_like(u), jnp.zeros_like(up), jnp.zeros_like(down)
+
+    up, down, up_in, down_in, pair = edges(u)
+    low_wrap = linked(up, wrap)
+    deriv_z, local_y, low, high = lax.cond(place == column - 1, skip, early, u, up_in, down_in, pair)
+    down, deriv_z, local_y, low, high = lax.optimization_barrier((down, deriv_z, local_y, low, high))
+    high_wrap = linked(down, back(wrap))
+    deriv_z, local_y = lax.cond(place == column - 1, lambda u, z, y: along_z(u), lambda u, z, y: (z, y), u, deriv_z, local_y)
+    pair, high, deriv_z, local_y = lax.optimization_barrier((pair, high, deriv_z, local_y))
+    high = lax.cond(place >= column - 2, lambda pair, high: linked(pair, final), lambda pair, high: high, pair, high)
+    deriv_y = join(local_y, low_wrap, low, high)
+    deriv_y = join_last(deriv_y, local_y, high, high_wrap)
     return deriv_y.reshape(shape), deriv_z.reshape(shape)
 
 

time: 29 us -> 26.5 us (0.914)
  the two profiles are of different devices: /device:TPU:15 before, /device:TPU:128 now
where the time goes in v3:
time: 26.5 us; the launch traced here: 26.3 us
  starting transfers between devices  18.7 us (71%)
  Pallas kernels  5.2 us (20%)
  waiting for transfers between devices  1.51 us (6%)
  between operations  0.75 us (3%)
    ppermute x1, starting transfers between devices, along_z(): there = lax.ppermute(pair, ('gy', 'gz'), links)  7.85 us
    ppermute x2, starting transfers between devices, shifted(): lax.ppermute(shard, axis, [(i, (i + by) % count) for i in range(count)])  6.11 us
    ppermute x4, starting transfers between devices, linked(): return lax.ppermute(shard, 'gy', pairs)  4.03 us
    ppermute x2, waiting for transfers between devices, shifted(): lax.ppermute(shard, axis, [(i, (i + by) % count) for i in range(count)])  1.5 us
    pallas_call x1, Pallas kernels, local_parts(): pl.pallas_call(local_kernel, out_shape=(out, out), in_specs=[here], out_s...  1.31 us
    pallas_call x1, Pallas kernels, join_z(): pl.pallas_call(join_z_kernel, out_shape=jax.ShapeDtypeStruct(local.shape,...  1.3 us
    pallas_call x1, Pallas kernels, edges(): pl.pallas_call(edges_kernel, out_shape=(out,) * 5, in_specs=[pl.BlockSpec...  1.13 us
    pallas_call x1, Pallas kernels, join(): pl.pallas_call(join_kernel, out_shape=jax.ShapeDtypeStruct(local.shape, j...  0.95 us
  transfers between devices with their start and end apart: 8, of which 1 were waited for; matrix products, arithmetic and copies ran while one was open for 0% of the time, Pallas kernels for 15%

profile of v3, /device:TPU:128, one launch (start us, length us, event | category | flops | bytes accessed | tf_op | source)
XLA Modules:
  0.0 26.3 jit_solution(2477735749575970842)
XLA Ops:
  0.6 0.0 copy-start
  0.6 1.1 %edges_y.1 = (f32[6,2,256]{2,1,0:T(2,128)S(1)}, f32[6,2,256]{2,1,0:T(2,128)S(1)}, f32[6,2,256]{2,1,0:T(2,128)S(1)}, f32[6,2,256]{2,1,0:T(2,128)S(1)}, f32[6,2,256]{2,1,0:T(2,128)S(1)}) custom-call(f32[6,64,256]{2,1,0:T(8,128)} %bitcast.3), custom_call_target="tpu_custom_call" | custom-call | tf_op jit(solution)/shard_map/edges_y/pallas_call | solution.py:71
  1.8 0.7 %collective-permute-start.9 = (f32[6,2,256]{2,1,0:T(2,128)S(1)}, f32[6,2,256]{2,1,0:T(2,128)S(1)}, u32[]{:S(2)}, u32[]{:S(2)}) collective-permute-start(f32[6,2,256]{2,1,0:T(2,128)S(1)} %get-tuple-element.86), channel_id=1, source_target_pairs={{112,128},{240,256},{368,384},{496,512},{624,640},{752,768},{880,8... | collective-permute-start | bytes 36872 | tf_op jit(solution)/shard_map/ppermute | solution.py:251
  2.5 0.0 copy-done
  2.5 22.0 %conditional.3 = (f32[6,64,256]{2,1,0:T(8,128)S(1)}, f32[6,64,256]{2,1,0:T(8,128)S(1)}, f32[6,2,256]{2,1,0:T(2,128)S(1)}, f32[6,2,256]{2,1,0:T(2,128)S(1)}) conditional(s32[]{:T(128)} %convert_element_type.7, (f32[6,2,256]{2,1,0:T(2,128)S(1)}, f32[6,64,256]{2,1,0:T(8,128)S(1)}, s32[]{:T(128)}, s32[]{:T(128)}, s32[]{:T(128)}, ...), branch_computations={%region_0.1_spmd, %region_1.2_spmd} | conditional | flops 100672512 | bytes 1474874 | solution.py:297
  2.5 0.7 %collective-permute-start.3 = (f32[6,2,256]{2,1,0:T(2,128)S(1)}, f32[6,2,256]{2,1,0:T(2,128)S(1)}, u32[]{:S(2)}, u32[]{:S(2)}) collective-permute-start(f32[6,2,256]{2,1,0:T(2,128)S(1)} %get-tuple-element.42), channel_id=1, source_target_pairs={{1,17},{2,18},{3,19},{4,20},{5,21},{6,22},{7,23},{8,24},{9,25},{10... | collective-permute-start | bytes 36872 | tf_op jit(solution)/shard_map/cond/branch_0_fun/ppermute | solution.py:284
  3.2 0.0 collective-permute-done.3
  3.2 0.4 %edges_z.2 = (f32[2,384]{1,0:T(2,128)S(1)}, f32[2,384]{1,0:T(2,128)S(1)}) custom-call(f32[6,64,256]{2,1,0:T(8,128)S(1)} %get-tuple-element.32.u_ref), custom_call_target="tpu_custom_call" | custom-call | tf_op jit(solution)/shard_map/cond/branch_0_fun/edges_z/pallas_call | solution.py:163
  3.6 6.1 %collective-permute-start.4 = (f32[2,384]{1,0:T(2,128)S(1)}, f32[2,384]{1,0:T(2,128)S(1)}, u32[]{:S(2)}, u32[]{:S(2)}) collective-permute-start(f32[2,384]{1,0:T(2,128)S(1)} %get-tuple-element.34), channel_id=1, source_target_pairs={{0,15},{1,0},{2,1},{3,2},{4,3},{5,4},{6,5},{7,6},{8,7},{9,8},{10,9... | collective-permute-start | bytes 9224 | tf_op jit(solution)/shard_map/cond/branch_0_fun/ppermute | solution.py:247
  9.7 0.0 collective-permute-start.5
  9.7 1.4 %collective-permute-start.7 = (f32[6,2,256]{2,1,0:T(2,128)S(1)}, f32[6,2,256]{2,1,0:T(2,128)S(1)}, u32[]{:S(2)}, u32[]{:S(2)}) collective-permute-start(f32[6,2,256]{2,1,0:T(2,128)S(1)} %get-tuple-element.44), channel_id=1, source_target_pairs={{16,32},{32,48},{48,64},{64,80},{80,96},{144,160},{160,176},{176,1... | collective-permute-start | bytes 36872 | tf_op jit(solution)/shard_map/cond/branch_0_fun/ppermute | solution.py:251
  11.1 1.3 %collective-permute-start.8 = (f32[6,2,256]{2,1,0:T(2,128)S(1)}, f32[6,2,256]{2,1,0:T(2,128)S(1)}, u32[]{:S(2)}, u32[]{:S(2)}) collective-permute-start(f32[6,2,256]{2,1,0:T(2,128)S(1)} %get-tuple-element.45), channel_id=1, source_target_pairs={{32,16},{48,32},{64,48},{80,64},{96,80},{160,144},{176,160},{192,1... | collective-permute-start | bytes 36872 | tf_op jit(solution)/shard_map/cond/branch_0_fun/ppermute | solution.py:251
  12.4 0.0 collective-permute-done.4.high_ref
  12.4 1.5 %collective-permute-done.5.low_ref = f32[2,384]{1,0:T(2,128)S(1)} collective-permute-done((f32[2,384]{1,0:T(2,128)S(1)}, f32[2,384]{1,0:T(2,128)S(1)}, u32[]{:S(2)}, u32[]{:S(2)}) %collective-permute-start.5) | collective-permute-done | bytes 3104 | tf_op jit(solution)/shard_map/cond/branch_0_fun/ppermute | solution.py:247
  13.9 7.9 %collective-permute-start.6 = (f32[6,2,256]{2,1,0:T(2,128)S(1)}, f32[6,2,256]{2,1,0:T(2,128)S(1)}, u32[]{:S(2)}, u32[]{:S(2)}) collective-permute-start(f32[6,2,256]{2,1,0:T(2,128)S(1)} %get-tuple-element.42), channel_id=1, source_target_pairs={{0,16},{16,0}} | collective-permute-start | bytes 36872 | tf_op jit(solution)/shard_map/cond/branch_0_fun/ppermute | solution.py:262
  21.8 1.3 %local_parts.2 = (f32[6,64,256]{2,1,0:T(8,128)S(1)}, f32[6,64,256]{2,1,0:T(8,128)S(1)}) custom-call(f32[6,64,256]{2,1,0:T(8,128)S(1)} %get-tuple-element.32.u_ref), custom_call_target="tpu_custom_call" | custom-call | flops 100663296 | bytes 1179648 | tf_op jit(solution)/shard_map/cond/branch_0_fun/local_parts/pallas_call | solution.py:185
  23.1 1.3 %join_z.2 = f32[6,64,256]{2,1,0:T(8,128)S(1)} custom-call(f32[6,64,256]{2,1,0:T(8,128)S(1)} %get-tuple-element.33.local_ref, f32[2,384]{1,0:T(2,128)S(1)} %collective-permute-done.4.high_ref, f32[2,384]{1,0:T(2,128)S(1)} %collective-permute-done.5.low_ref), custom_call_target="tpu_custom_call" | custom-call | tf_op jit(solution)/shard_map/cond/branch_0_fun/join_z/pallas_call | solution.py:219
  24.4 0.0 collective-permute-done.7
  24.5 0.0 collective-permute-done.8
  24.5 0.0 collective-permute-done.6
  24.5 0.7 %collective-permute-start.10 = (f32[6,2,256]{2,1,0:T(2,128)S(1)}, f32[6,2,256]{2,1,0:T(2,128)S(1)}, u32[]{:S(2)}, u32[]{:S(2)}) collective-permute-start(f32[6,2,256]{2,1,0:T(2,128)S(1)} %get-tuple-element.90), channel_id=1, source_target_pairs={{128,112},{256,240},{384,368},{512,496},{640,624},{768,752},{896,8... | collective-permute-start | bytes 36872 | tf_op jit(solution)/shard_map/ppermute | solution.py:251
  25.2 0.0 copy-start.1
  25.2 0.0 collective-permute-done.9.wrap_ref
  25.2 0.9 %join_y.1.made_hbm = f32[6,64,256]{2,1,0:T(8,128)} custom-call(f32[6,64,256]{2,1,0:T(8,128)S(1)} %get-tuple-element.85.local_ref, f32[6,2,256]{2,1,0:T(2,128)S(1)} %collective-permute-done.9.wrap_ref, f32[6,2,256]{2,1,0:T(2,128)S(1)} %get-tuple-element.87.low_ref, f32[6,2,256]{2,1,0:T(2,128)S(1)} %get-tuple-element.107.high_ref.low_ref), custom_call_target="tpu_custom_call" | custom-call | flops 589824 | bytes 786432 | tf_op jit(solution)/shard_map/join_y/pallas_call | solution.py:118
  26.2 0.0 copy-done.1
  26.2 0.0 collective-permute-done.10.wrap_ref
  26.2 0.1 join_y_last.1
  (3 shorter events, 0.0 us)
Async XLA Ops:
  0.6 1.8 %copy-start = (f32[3,2,64,256]{3,2,1,0:T(8,128)S(1)}, f32[3,2,64,256]{3,2,1,0:T(8,128)}, u32[]{:S(2)}) copy-start(f32[3,2,64,256]{3,2,1,0:T(8,128)} %param.7) | copy-start | bytes 1179652
  1.8 23.5 %collective-permute-start.9 = (f32[6,2,256]{2,1,0:T(2,128)S(1)}, f32[6,2,256]{2,1,0:T(2,128)S(1)}, u32[]{:S(2)}, u32[]{:S(2)}) collective-permute-start(f32[6,2,256]{2,1,0:T(2,128)S(1)} %get-tuple-element.86), channel_id=1, source_target_pairs={{112,128},{240,256},{368,384},{496,512},{624,640},{752,768},{880,8... | collective-permute-start | bytes 36872 | tf_op jit(solution)/shard_map/ppermute | solution.py:251
  2.5 0.7 %collective-permute-start.3 = (f32[6,2,256]{2,1,0:T(2,128)S(1)}, f32[6,2,256]{2,1,0:T(2,128)S(1)}, u32[]{:S(2)}, u32[]{:S(2)}) collective-permute-start(f32[6,2,256]{2,1,0:T(2,128)S(1)} %get-tuple-element.42), channel_id=1, source_target_pairs={{1,17},{2,18},{3,19},{4,20},{5,21},{6,22},{7,23},{8,24},{9,25},{10... | collective-permute-start | bytes 36872 | tf_op jit(solution)/shard_map/cond/branch_0_fun/ppermute | solution.py:284
  3.6 8.8 %collective-permute-start.4 = (f32[2,384]{1,0:T(2,128)S(1)}, f32[2,384]{1,0:T(2,128)S(1)}, u32[]{:S(2)}, u32[]{:S(2)}) collective-permute-start(f32[2,384]{1,0:T(2,128)S(1)} %get-tuple-element.34), channel_id=1, source_target_pairs={{0,15},{1,0},{2,1},{3,2},{4,3},{5,4},{6,5},{7,6},{8,7},{9,8},{10,9... | collective-permute-start | bytes 9224 | tf_op jit(solution)/shard_map/cond/branch_0_fun/ppermute | solution.py:247
  9.7 4.2 %collective-permute-start.5 = (f32[2,384]{1,0:T(2,128)S(1)}, f32[2,384]{1,0:T(2,128)S(1)}, u32[]{:S(2)}, u32[]{:S(2)}) collective-permute-start(f32[2,384]{1,0:T(2,128)S(1)} %get-tuple-element.35), channel_id=1, source_target_pairs={{0,1},{1,2},{2,3},{3,4},{4,5},{5,6},{6,7},{7,8},{8,9},{9,10},{10,1... | collective-permute-start | bytes 9224 | tf_op jit(solution)/shard_map/cond/branch_0_fun/ppermute | solution.py:247
  9.7 14.7 %collective-permute-start.7 = (f32[6,2,256]{2,1,0:T(2,128)S(1)}, f32[6,2,256]{2,1,0:T(2,128)S(1)}, u32[]{:S(2)}, u32[]{:S(2)}) collective-permute-start(f32[6,2,256]{2,1,0:T(2,128)S(1)} %get-tuple-element.44), channel_id=1, source_target_pairs={{16,32},{32,48},{48,64},{64,80},{80,96},{144,160},{160,176},{176,1... | collective-permute-start | bytes 36872 | tf_op jit(solution)/shard_map/cond/branch_0_fun/ppermute | solution.py:251
  11.1 13.3 %collective-permute-start.8 = (f32[6,2,256]{2,1,0:T(2,128)S(1)}, f32[6,2,256]{2,1,0:T(2,128)S(1)}, u32[]{:S(2)}, u32[]{:S(2)}) collective-permute-start(f32[6,2,256]{2,1,0:T(2,128)S(1)} %get-tuple-element.45), channel_id=1, source_target_pairs={{32,16},{48,32},{64,48},{80,64},{96,80},{160,144},{176,160},{192,1... | collective-permute-start | bytes 36872 | tf_op jit(solution)/shard_map/cond/branch_0_fun/ppermute | solution.py:251
  13.9 10.5 %collective-permute-start.6 = (f32[6,2,256]{2,1,0:T(2,128)S(1)}, f32[6,2,256]{2,1,0:T(2,128)S(1)}, u32[]{:S(2)}, u32[]{:S(2)}) collective-permute-start(f32[6,2,256]{2,1,0:T(2,128)S(1)} %get-tuple-element.42), channel_id=1, source_target_pairs={{0,16},{16,0}} | collective-permute-start | bytes 36872 | tf_op jit(solution)/shard_map/cond/branch_0_fun/ppermute | solution.py:262
  24.5 1.7 %collective-permute-start.10 = (f32[6,2,256]{2,1,0:T(2,128)S(1)}, f32[6,2,256]{2,1,0:T(2,128)S(1)}, u32[]{:S(2)}, u32[]{:S(2)}) collective-permute-start(f32[6,2,256]{2,1,0:T(2,128)S(1)} %get-tuple-element.90), channel_id=1, source_target_pairs={{128,112},{256,240},{384,368},{512,496},{640,624},{768,752},{896,8... | collective-permute-start | bytes 36872 | tf_op jit(solution)/shard_map/ppermute | solution.py:251
  25.2 1.0 %copy-start.1 = (f32[6,64,256]{2,1,0:T(8,128)}, f32[6,64,256]{2,1,0:T(8,128)S(1)}, u32[]{:S(2)}) copy-start(f32[6,64,256]{2,1,0:T(8,128)S(1)} %get-tuple-element.91) | copy-start | bytes 1179652

commit v4 on v3

--- a/solution.py
+++ b/solution.py
@@ -39,7 +39,7 @@
     return jnp.where(lag == 0, 0.0, jnp.where(lag > 0, weight, -weight))
 
 
-def edges_kernel(u_hbm, up_ref, down_ref, up_in_ref, down_in_ref, pair_ref, u_ref, sem):
+def edges_kernel(u_hbm, u_ref, up_ref, down_ref, up_in_ref, down_in_ref, pair_ref, sem):
     planes, ny, nz = u_ref.shape
     even = lax.axis_index("gy") % 2 == 0
     copies = [pltpu.make_async_copy(u_hbm.at[p], u_ref.at[p], sem.at[p]) for p in range(planes)]
@@ -70,13 +70,13 @@
     out = pltpu.VMEM((planes, 2, nz), jnp.float32)
     return pl.pallas_call(
         edges_kernel,
-        out_shape=(out,) * 5,
+        out_shape=(pltpu.VMEM(u.shape, jnp.float32),) + (out,) * 5,
         in_specs=[pl.BlockSpec(memory_space=pl.ANY)],
-        out_specs=(pl.BlockSpec(memory_space=pltpu.VMEM),) * 5,
-        scratch_shapes=[pltpu.VMEM(u.shape, jnp.float32), pltpu.SemaphoreType.DMA((planes,))],
+        out_specs=(pl.BlockSpec(memory_space=pltpu.VMEM),) * 6,
+        scratch_shapes=[pltpu.SemaphoreType.DMA((planes,))],
         compiler_params=pltpu.CompilerParams(vmem_limit_bytes=vmem),
         name="edges_y",
-    )(u)
+    )(pltpu.with_memory_space_constraint(u, pltpu.HBM))
 
 
 def join_rows(local_ref, low_of, high_of, out_hbm, out_ref, sem):
@@ -172,10 +172,11 @@
 
 def local_kernel(u_ref, z_ref, y_ref):
     planes, ny, nz = u_ref.shape
-    along = operator((nz, nz), 0, 1)
+    lines = u_ref[...].reshape(planes * ny, nz)
     across = operator((ny, ny), 0, 0)
+    along_z = jnp.dot(lines, operator((nz, nz), 0, 1), precision=best, preferred_element_type=jnp.float32)
+    z_ref[...] = along_z.reshape(planes, ny, nz)
     for p in range(planes):
-        z_ref[p] = jnp.dot(u_ref[p], along, precision=best, preferred_element_type=jnp.float32)
         y_ref[p] = jnp.dot(across, u_ref[p], precision=best, preferred_element_type=jnp.float32)
 
 
@@ -193,7 +194,7 @@
     )(u)
 
 
-def join_z_kernel(local_ref, high_ref, low_ref, out_hbm, out_ref, sem):
+def join_z_kernel(local_ref, high_ref, low_ref, out_ref):
     planes, ny, nz = local_ref.shape
     ends = jnp.concatenate([low_ref[...], high_ref[...], low_ref[...], high_ref[...]], axis=0)
     ends = jnp.transpose(ends)
@@ -202,26 +203,20 @@
     low_rest = jnp.where(cell == 0, 0.0, decay(jnp.maximum(cell - 1, 0)))
     high_first = jnp.where(cell == nz - 1, 1.0, 0.0)
     high_rest = jnp.where(cell == nz - 1, 0.0, decay(jnp.maximum(nz - 2 - cell, 0)))
-    copies = []
     for p in range(planes):
         end = ends[p * ny : (p + 1) * ny]
         low = end[:, 0:1] * low_first + end[:, 1:2] * low_rest
         high = end[:, 2:3] * high_rest + end[:, 3:4] * high_first
         out_ref[p] = local_ref[p] + low + high
-        copies.append(pltpu.make_async_copy(out_ref.at[p], out_hbm.at[p], sem.at[p]))
-        copies[p].start()
-    for copy in copies:
-        copy.wait()
 
 
 def join_z(local, low, high):
-    planes = local.shape[0]
+    here = pl.BlockSpec(memory_space=pltpu.VMEM)
     return pl.pallas_call(
         join_z_kernel,
         out_shape=jax.ShapeDtypeStruct(local.shape, jnp.float32),
-        in_specs=[pl.BlockSpec(memory_space=pltpu.VMEM)] * 3,
-        out_specs=pl.BlockSpec(memory_space=pl.ANY),
-        scratch_shapes=[pltpu.VMEM(local.shape, jnp.float32), pltpu.SemaphoreType.DMA((planes,))],
+        in_specs=[here] * 3,
+        out_specs=here,
         compiler_params=pltpu.CompilerParams(vmem_limit_bytes=vmem),
         name="join_z",
     )(local, high, low)
@@ -251,16 +246,12 @@
     return lax.ppermute(shard, "gy", pairs)
 
 
-def along_z(u, pair=None, links=None):
+def along_z(u):
     up, down = edges_z(u)
     high = shifted(down, "gz", -1)
     low = shifted(up, "gz", 1)
     local_z, local_y = local_parts(u)
-    if links is None:
-        return join_z(local_z, low, high), local_y
-    high, low, pair = lax.optimization_barrier((high, low, pair))
-    there = lax.ppermute(pair, ("gy", "gz"), links)
-    return join_z(local_z, low, high), local_y, there
+    return join_z(local_z, low, high), local_y
 
 
 def per_device(velocity):
@@ -284,15 +275,16 @@
         pair_in = lax.ppermute(pair, ("gy", "gz"), first)
         low = linked(up, inner)
         high = linked(down, back(inner))
-        u, pair_in = lax.optimization_barrier((u, pair_in))
-        deriv_z, local_y, there = along_z(u, pair, last)
-        pair_in = jnp.where(slow, there, pair_in)
+        u, pair, pair_in = lax.optimization_barrier((u, pair, pair_in))
+        u, high = lax.optimization_barrier((u, high))
+        deriv_z, local_y = along_z(u)
+        pair_in = jnp.where(slow, lax.ppermute(pair, ("gy", "gz"), last), pair_in)
         return deriv_z, local_y, jnp.where(place == 1, pair_in, low), jnp.where(place == 0, pair_in, high)
 
     def skip(u, up, down, pair):
         return place_z(u), jnp.zeros_like(u), jnp.zeros_like(up), jnp.zeros_like(down)
 
-    up, down, up_in, down_in, pair = edges(u)
+    u, up, down, up_in, down_in, pair = edges(u)
     low_wrap = linked(up, wrap)
     deriv_z, local_y, low, high = lax.cond(place == column - 1, skip, early, u, up_in, down_in, pair)
     down, deriv_z, local_y, low, high = lax.optimization_barrier((down, deriv_z, local_y, low, high))

time: 26.5 us -> 26.1 us (0.985)
  the two profiles are of different devices: /device:TPU:128 before, /device:TPU:1 now
where the time goes in v4:
time: 26.1 us; the launch traced here: 25.8 us
  starting transfers between devices  20.8 us (80%)
  Pallas kernels  3.98 us (15%)
  between operations  0.74 us (3%)
    ppermute x2, starting transfers between devices, shifted(): lax.ppermute(shard, axis, [(i, (i + by) % count) for i in range(count)])  11 us
    ppermute x1, starting transfers between devices, early(): pair_in = lax.ppermute(pair, ('gy', 'gz'), first)  5.11 us
    ppermute x4, starting transfers between devices, linked(): return lax.ppermute(shard, 'gy', pairs)  4 us
    pallas_call x1, Pallas kernels, edges(): pl.pallas_call(edges_kernel, out_shape=(pltpu.VMEM(u.shape, jnp.float32),...  1.08 us
    pallas_call x1, Pallas kernels, local_parts(): pl.pallas_call(local_kernel, out_shape=(out, out), in_specs=[here], out_s...  1.01 us
    pallas_call x1, Pallas kernels, join(): pl.pallas_call(join_kernel, out_shape=jax.ShapeDtypeStruct(local.shape, j...  0.95 us
    ppermute x1, starting transfers between devices, early(): pair_in = jnp.where(slow, lax.ppermute(pair, ('gy', 'gz'), last), pair_in)  0.66 us
  transfers between devices with their start and end apart: 8, of which 1 were waited for; matrix products, arithmetic and copies ran while one was open for 0% of the time, Pallas kernels for 11%

profile of v4, /device:TPU:1, one launch (start us, length us, event | category | flops | bytes accessed | tf_op | source)
XLA Modules:
  0.0 25.8 jit_solution(17343248771660918743)
XLA Ops:
  0.6 1.1 %edges_y.1 = (f32[6,64,256]{2,1,0:T(8,128)S(1)}, f32[6,2,256]{2,1,0:T(2,128)S(1)}, f32[6,2,256]{2,1,0:T(2,128)S(1)}, f32[6,2,256]{2,1,0:T(2,128)S(1)}, f32[6,2,2...) custom-call(f32[6,64,256]{2,1,0:T(8,128)} %bitcast.4), custom_call_target="tpu_custom_call" | custom-call | tf_op jit(solution)/shard_map/edges_y/pallas_call | solution.py:71
  1.7 1.3 %collective-permute-start.9 = (f32[6,2,256]{2,1,0:T(2,128)S(1)}, f32[6,2,256]{2,1,0:T(2,128)S(1)}, u32[]{:S(2)}, u32[]{:S(2)}) collective-permute-start(f32[6,2,256]{2,1,0:T(2,128)S(1)} %get-tuple-element.88), channel_id=1, source_target_pairs={{112,128},{240,256},{368,384},{496,512},{624,640},{752,768},{880,8... | collective-permute-start | bytes 36872 | tf_op jit(solution)/shard_map/ppermute | solution.py:246
  3.0 20.3 %conditional.3 = (f32[6,64,256]{2,1,0:T(8,128)S(1)}, f32[6,64,256]{2,1,0:T(8,128)S(1)}, f32[6,2,256]{2,1,0:T(2,128)S(1)}, f32[6,2,256]{2,1,0:T(2,128)S(1)}) conditional(s32[]{:T(128)} %convert_element_type.7, (f32[6,2,256]{2,1,0:T(2,128)S(1)}, f32[6,64,256]{2,1,0:T(8,128)S(1)}, f32[6,2,256]{2,1,0:T(2,128)S(1)}, s32[]{:T(128)}, s32[]{:T(128)}, ...), branch_computations={%region_0.1_spmd, %region_1.2_spmd} | conditional | flops 100672512 | bytes 1474874 | solution.py:289
  3.0 5.1 %collective-permute-start.3 = (f32[6,2,256]{2,1,0:T(2,128)S(1)}, f32[6,2,256]{2,1,0:T(2,128)S(1)}, u32[]{:S(2)}, u32[]{:S(2)}) collective-permute-start(f32[6,2,256]{2,1,0:T(2,128)S(1)} %get-tuple-element.42), channel_id=1, source_target_pairs={{1,17},{2,18},{3,19},{4,20},{5,21},{6,22},{7,23},{8,24},{9,25},{10... | collective-permute-start | bytes 36872 | tf_op jit(solution)/shard_map/cond/branch_0_fun/ppermute | solution.py:275
  8.2 0.7 %collective-permute-start.4 = (f32[6,2,256]{2,1,0:T(2,128)S(1)}, f32[6,2,256]{2,1,0:T(2,128)S(1)}, u32[]{:S(2)}, u32[]{:S(2)}) collective-permute-start(f32[6,2,256]{2,1,0:T(2,128)S(1)} %get-tuple-element.33), channel_id=1, source_target_pairs={{32,16},{48,32},{64,48},{80,64},{96,80},{160,144},{176,160},{192,1... | collective-permute-start | bytes 36872 | tf_op jit(solution)/shard_map/cond/branch_0_fun/ppermute | solution.py:246
  8.8 0.7 %collective-permute-start.8 = (f32[6,2,256]{2,1,0:T(2,128)S(1)}, f32[6,2,256]{2,1,0:T(2,128)S(1)}, u32[]{:S(2)}, u32[]{:S(2)}) collective-permute-start(f32[6,2,256]{2,1,0:T(2,128)S(1)} %get-tuple-element.44), channel_id=1, source_target_pairs={{16,32},{32,48},{48,64},{64,80},{80,96},{144,160},{160,176},{176,1... | collective-permute-start | bytes 36872 | tf_op jit(solution)/shard_map/cond/branch_0_fun/ppermute | solution.py:246
  9.5 0.0 collective-permute-done.3
  9.5 0.7 %collective-permute-start.7 = (f32[6,2,256]{2,1,0:T(2,128)S(1)}, f32[6,2,256]{2,1,0:T(2,128)S(1)}, u32[]{:S(2)}, u32[]{:S(2)}) collective-permute-start(f32[6,2,256]{2,1,0:T(2,128)S(1)} %get-tuple-element.42), channel_id=1, source_target_pairs={{0,16},{16,0}} | collective-permute-start | bytes 36872 | tf_op jit(solution)/shard_map/cond/branch_0_fun/ppermute | solution.py:281
  10.2 0.0 collective-permute-done.4
  10.2 0.4 %edges_z.2 = (f32[2,384]{1,0:T(2,128)S(1)}, f32[2,384]{1,0:T(2,128)S(1)}) custom-call(f32[6,64,256]{2,1,0:T(8,128)S(1)} %get-tuple-element.34.u_ref), custom_call_target="tpu_custom_call" | custom-call | tf_op jit(solution)/shard_map/cond/branch_0_fun/edges_z/pallas_call | solution.py:163
  10.6 11.0 %collective-permute-start.5 = (f32[2,384]{1,0:T(2,128)S(1)}, f32[2,384]{1,0:T(2,128)S(1)}, u32[]{:S(2)}, u32[]{:S(2)}) collective-permute-start(f32[2,384]{1,0:T(2,128)S(1)} %get-tuple-element.36), channel_id=1, source_target_pairs={{0,15},{1,0},{2,1},{3,2},{4,3},{5,4},{6,5},{7,6},{8,7},{9,8},{10,9... | collective-permute-start | bytes 9224 | tf_op jit(solution)/shard_map/cond/branch_0_fun/ppermute | solution.py:242
  21.6 0.0 collective-permute-start.6
  21.6 1.0 %local_parts.2 = (f32[6,64,256]{2,1,0:T(8,128)S(1)}, f32[6,64,256]{2,1,0:T(8,128)S(1)}) custom-call(f32[6,64,256]{2,1,0:T(8,128)S(1)} %get-tuple-element.34.u_ref), custom_call_target="tpu_custom_call" | custom-call | flops 100663296 | bytes 1179648 | tf_op jit(solution)/shard_map/cond/branch_0_fun/local_parts/pallas_call | solution.py:186
  22.7 0.0 collective-permute-done.5.high_ref
  22.7 0.1 collective-permute-done.6.low_ref
  22.8 0.4 %join_z.2 = f32[6,64,256]{2,1,0:T(8,128)S(1)} custom-call(f32[6,64,256]{2,1,0:T(8,128)S(1)} %get-tuple-element.35.local_ref, f32[2,384]{1,0:T(2,128)S(1)} %collective-permute-done.5.high_ref, f32[2,384]{1,0:T(2,128)S(1)} %collective-permute-done.6.low_ref), custom_call_target="tpu_custom_call" | custom-call | tf_op jit(solution)/shard_map/cond/branch_0_fun/join_z/pallas_call | solution.py:215
  23.2 0.0 collective-permute-done.8
  23.2 0.0 collective-permute-done.7
  23.3 1.4 %collective-permute-start.10 = (f32[6,2,256]{2,1,0:T(2,128)S(1)}, f32[6,2,256]{2,1,0:T(2,128)S(1)}, u32[]{:S(2)}, u32[]{:S(2)}) collective-permute-start(f32[6,2,256]{2,1,0:T(2,128)S(1)} %get-tuple-element.92), channel_id=1, source_target_pairs={{128,112},{256,240},{384,368},{512,496},{640,624},{768,752},{896,8... | collective-permute-start | bytes 36872 | tf_op jit(solution)/shard_map/ppermute | solution.py:246
  24.7 0.0 copy-start
  24.7 0.0 collective-permute-done.9.wrap_ref
  24.8 0.9 %join_y.1.made_hbm = f32[6,64,256]{2,1,0:T(8,128)} custom-call(f32[6,64,256]{2,1,0:T(8,128)S(1)} %get-tuple-element.87.local_ref, f32[6,2,256]{2,1,0:T(2,128)S(1)} %collective-permute-done.9.wrap_ref, f32[6,2,256]{2,1,0:T(2,128)S(1)} %get-tuple-element.89.low_ref, f32[6,2,256]{2,1,0:T(2,128)S(1)} %get-tuple-element.109.high_ref.low_ref), custom_call_target="tpu_custom_call" | custom-call | flops 589824 | bytes 786432 | tf_op jit(solution)/shard_map/join_y/pallas_call | solution.py:118
  25.7 0.0 copy-done
  25.7 0.0 collective-permute-done.10.wrap_ref
  25.7 0.1 join_y_last.1
  (3 shorter events, 0.0 us)
Async XLA Ops:
  1.7 23.0 %collective-permute-start.9 = (f32[6,2,256]{2,1,0:T(2,128)S(1)}, f32[6,2,256]{2,1,0:T(2,128)S(1)}, u32[]{:S(2)}, u32[]{:S(2)}) collective-permute-start(f32[6,2,256]{2,1,0:T(2,128)S(1)} %get-tuple-element.88), channel_id=1, source_target_pairs={{112,128},{240,256},{368,384},{496,512},{624,640},{752,768},{880,8... | collective-permute-start | bytes 36872 | tf_op jit(solution)/shard_map/ppermute | solution.py:246
  3.0 6.5 %collective-permute-start.3 = (f32[6,2,256]{2,1,0:T(2,128)S(1)}, f32[6,2,256]{2,1,0:T(2,128)S(1)}, u32[]{:S(2)}, u32[]{:S(2)}) collective-permute-start(f32[6,2,256]{2,1,0:T(2,128)S(1)} %get-tuple-element.42), channel_id=1, source_target_pairs={{1,17},{2,18},{3,19},{4,20},{5,21},{6,22},{7,23},{8,24},{9,25},{10... | collective-permute-start | bytes 36872 | tf_op jit(solution)/shard_map/cond/branch_0_fun/ppermute | solution.py:275
  8.2 2.0 %collective-permute-start.4 = (f32[6,2,256]{2,1,0:T(2,128)S(1)}, f32[6,2,256]{2,1,0:T(2,128)S(1)}, u32[]{:S(2)}, u32[]{:S(2)}) collective-permute-start(f32[6,2,256]{2,1,0:T(2,128)S(1)} %get-tuple-element.33), channel_id=1, source_target_pairs={{32,16},{48,32},{64,48},{80,64},{96,80},{160,144},{176,160},{192,1... | collective-permute-start | bytes 36872 | tf_op jit(solution)/shard_map/cond/branch_0_fun/ppermute | solution.py:246
  8.8 14.4 %collective-permute-start.8 = (f32[6,2,256]{2,1,0:T(2,128)S(1)}, f32[6,2,256]{2,1,0:T(2,128)S(1)}, u32[]{:S(2)}, u32[]{:S(2)}) collective-permute-start(f32[6,2,256]{2,1,0:T(2,128)S(1)} %get-tuple-element.44), channel_id=1, source_target_pairs={{16,32},{32,48},{48,64},{64,80},{80,96},{144,160},{160,176},{176,1... | collective-permute-start | bytes 36872 | tf_op jit(solution)/shard_map/cond/branch_0_fun/ppermute | solution.py:246
  9.5 13.7 %collective-permute-start.7 = (f32[6,2,256]{2,1,0:T(2,128)S(1)}, f32[6,2,256]{2,1,0:T(2,128)S(1)}, u32[]{:S(2)}, u32[]{:S(2)}) collective-permute-start(f32[6,2,256]{2,1,0:T(2,128)S(1)} %get-tuple-element.42), channel_id=1, source_target_pairs={{0,16},{16,0}} | collective-permute-start | bytes 36872 | tf_op jit(solution)/shard_map/cond/branch_0_fun/ppermute | solution.py:281
  10.6 12.0 %collective-permute-start.5 = (f32[2,384]{1,0:T(2,128)S(1)}, f32[2,384]{1,0:T(2,128)S(1)}, u32[]{:S(2)}, u32[]{:S(2)}) collective-permute-start(f32[2,384]{1,0:T(2,128)S(1)} %get-tuple-element.36), channel_id=1, source_target_pairs={{0,15},{1,0},{2,1},{3,2},{4,3},{5,4},{6,5},{7,6},{8,7},{9,8},{10,9... | collective-permute-start | bytes 9224 | tf_op jit(solution)/shard_map/cond/branch_0_fun/ppermute | solution.py:242
  21.6 1.2 %collective-permute-start.6 = (f32[2,384]{1,0:T(2,128)S(1)}, f32[2,384]{1,0:T(2,128)S(1)}, u32[]{:S(2)}, u32[]{:S(2)}) collective-permute-start(f32[2,384]{1,0:T(2,128)S(1)} %get-tuple-element.37), channel_id=1, source_target_pairs={{0,1},{1,2},{2,3},{3,4},{4,5},{5,6},{6,7},{7,8},{8,9},{9,10},{10,1... | collective-permute-start | bytes 9224 | tf_op jit(solution)/shard_map/cond/branch_0_fun/ppermute | solution.py:242
  23.3 2.4 %collective-permute-start.10 = (f32[6,2,256]{2,1,0:T(2,128)S(1)}, f32[6,2,256]{2,1,0:T(2,128)S(1)}, u32[]{:S(2)}, u32[]{:S(2)}) collective-permute-start(f32[6,2,256]{2,1,0:T(2,128)S(1)} %get-tuple-element.92), channel_id=1, source_target_pairs={{128,112},{256,240},{384,368},{512,496},{640,624},{768,752},{896,8... | collective-permute-start | bytes 36872 | tf_op jit(solution)/shard_map/ppermute | solution.py:246
  24.7 1.0 %copy-start = (f32[6,64,256]{2,1,0:T(8,128)}, f32[6,64,256]{2,1,0:T(8,128)S(1)}, u32[]{:S(2)}) copy-start(f32[6,64,256]{2,1,0:T(8,128)S(1)} %get-tuple-element.93) | copy-start | bytes 1179652

commit v5 on v4

--- a/solution.py
+++ b/solution.py
@@ -180,7 +180,7 @@
         y_ref[p] = jnp.dot(across, u_ref[p], precision=best, preferred_element_type=jnp.float32)
 
 
-def local_parts(u):
+def local_parts(u, flops):
     out = jax.ShapeDtypeStruct(u.shape, jnp.float32)
     here = pl.BlockSpec(memory_space=pltpu.VMEM)
     return pl.pallas_call(
@@ -189,7 +189,7 @@
         in_specs=[here],
         out_specs=(here, here),
         compiler_params=pltpu.CompilerParams(vmem_limit_bytes=vmem),
-        cost_estimate=pl.CostEstimate(flops=2 * u.size * 512, bytes_accessed=12 * u.size, transcendentals=70000),
+        cost_estimate=pl.CostEstimate(flops=flops, bytes_accessed=12 * u.size, transcendentals=70000),
         name="local_parts",
     )(u)
 
@@ -246,11 +246,11 @@
     return lax.ppermute(shard, "gy", pairs)
 
 
-def along_z(u):
+def along_z(u, flops):
     up, down = edges_z(u)
     high = shifted(down, "gz", -1)
     low = shifted(up, "gz", 1)
-    local_z, local_y = local_parts(u)
+    local_z, local_y = local_parts(u, flops)
     return join_z(local_z, low, high), local_y
 
 
@@ -277,7 +277,7 @@
         high = linked(down, back(inner))
         u, pair, pair_in = lax.optimization_barrier((u, pair, pair_in))
         u, high = lax.optimization_barrier((u, high))
-        deriv_z, local_y = along_z(u)
+        deriv_z, local_y = along_z(u, 10**9)
         pair_in = jnp.where(slow, lax.ppermute(pair, ("gy", "gz"), last), pair_in)
         return deriv_z, local_y, jnp.where(place == 1, pair_in, low), jnp.where(place == 0, pair_in, high)
 
@@ -289,7 +289,7 @@
     deriv_z, local_y, low, high = lax.cond(place == column - 1, skip, early, u, up_in, down_in, pair)
     down, deriv_z, local_y, low, high = lax.optimization_barrier((down, deriv_z, local_y, low, high))
     high_wrap = linked(down, back(wrap))
-    deriv_z, local_y = lax.cond(place == column - 1, lambda u, z, y: along_z(u), lambda u, z, y: (z, y), u, deriv_z, local_y)
+    deriv_z, local_y = lax.cond(place == column - 1, lambda u, z, y: along_z(u, 10**8), lambda u, z, y: (z, y), u, deriv_z, local_y)
     pair, high, deriv_z, local_y = lax.optimization_barrier((pair, high, deriv_z, local_y))
     high = lax.cond(place >= column - 2, lambda pair, high: linked(pair, final), lambda pair, high: high, pair, high)
     deriv_y = join(local_y, low_wrap, low, high)

time: 26.1 us -> 26.1 us (level)
    ppermute x4, starting transfers between devices: 4 us -> 5.39 us  [linked(): return lax.ppermute(shard, 'gy', pairs)]
    ppermute x2, starting transfers between devices: 11 us -> 9.75 us  [shifted(): lax.ppermute(shard, axis, [(i, (i + by) % count) for i in range(count)])]
  transfers between devices with their start and end apart: 8 -> 8, of which waited for: 1 -> 0; matrix products, arithmetic and copies ran while one was open for 0% -> 0% of each run, Pallas kernels for 11% -> 11%
where the time goes in v5:
time: 26.1 us; the launch traced here: 25.8 us
  starting transfers between devices  20.9 us (80%)
  Pallas kernels  3.98 us (15%)
  between operations  0.74 us (3%)
    ppermute x2, starting transfers between devices, shifted(): lax.ppermute(shard, axis, [(i, (i + by) % count) for i in range(count)])  9.75 us
    ppermute x4, starting transfers between devices, linked(): return lax.ppermute(shard, 'gy', pairs)  5.39 us
    ppermute x1, starting transfers between devices, early(): pair_in = lax.ppermute(pair, ('gy', 'gz'), first)  5.11 us
    pallas_call x1, Pallas kernels, edges(): pl.pallas_call(edges_kernel, out_shape=(pltpu.VMEM(u.shape, jnp.float32),...  1.08 us
    pallas_call x1, Pallas kernels, local_parts(): pl.pallas_call(local_kernel, out_shape=(out, out), in_specs=[here], out_s...  1.01 us
    pallas_call x1, Pallas kernels, join(): pl.pallas_call(join_kernel, out_shape=jax.ShapeDtypeStruct(local.shape, j...  0.95 us
    ppermute x1, starting transfers between devices, early(): pair_in = jnp.where(slow, lax.ppermute(pair, ('gy', 'gz'), last), pair_in)  0.65 us
  transfers between devices with their start and end apart: 8, of which 0 were waited for; matrix products, arithmetic and copies ran while one was open for 0% of the time, Pallas kernels for 11%

profile of v5, /device:TPU:1, one launch (start us, length us, event | category | flops | bytes accessed | tf_op | source)
XLA Modules:
  0.0 25.8 jit_solution(13421042930228881147)
XLA Ops:
  0.6 1.1 %edges_y.1 = (f32[6,64,256]{2,1,0:T(8,128)S(1)}, f32[6,2,256]{2,1,0:T(2,128)S(1)}, f32[6,2,256]{2,1,0:T(2,128)S(1)}, f32[6,2,256]{2,1,0:T(2,128)S(1)}, f32[6,2,2...) custom-call(f32[6,64,256]{2,1,0:T(8,128)} %bitcast.4), custom_call_target="tpu_custom_call" | custom-call | tf_op jit(solution)/shard_map/edges_y/pallas_call | solution.py:71
  1.7 1.3 %collective-permute-start.9 = (f32[6,2,256]{2,1,0:T(2,128)S(1)}, f32[6,2,256]{2,1,0:T(2,128)S(1)}, u32[]{:S(2)}, u32[]{:S(2)}) collective-permute-start(f32[6,2,256]{2,1,0:T(2,128)S(1)} %get-tuple-element.88), channel_id=1, source_target_pairs={{112,128},{240,256},{368,384},{496,512},{624,640},{752,768},{880,8... | collective-permute-start | bytes 36872 | tf_op jit(solution)/shard_map/ppermute | solution.py:246
  3.0 18.9 %conditional.3 = (f32[6,64,256]{2,1,0:T(8,128)S(1)}, f32[6,64,256]{2,1,0:T(8,128)S(1)}, f32[6,2,256]{2,1,0:T(2,128)S(1)}, f32[6,2,256]{2,1,0:T(2,128)S(1)}) conditional(s32[]{:T(128)} %convert_element_type.7, (f32[6,2,256]{2,1,0:T(2,128)S(1)}, f32[6,64,256]{2,1,0:T(8,128)S(1)}, f32[6,2,256]{2,1,0:T(2,128)S(1)}, s32[]{:T(128)}, s32[]{:T(128)}, ...), branch_computations={%region_0.1_spmd, %region_1.2_spmd} | conditional | flops 1000009216 | bytes 1474874 | solution.py:289
  3.0 5.1 %collective-permute-start.3 = (f32[6,2,256]{2,1,0:T(2,128)S(1)}, f32[6,2,256]{2,1,0:T(2,128)S(1)}, u32[]{:S(2)}, u32[]{:S(2)}) collective-permute-start(f32[6,2,256]{2,1,0:T(2,128)S(1)} %get-tuple-element.42), channel_id=1, source_target_pairs={{1,17},{2,18},{3,19},{4,20},{5,21},{6,22},{7,23},{8,24},{9,25},{10... | collective-permute-start | bytes 36872 | tf_op jit(solution)/shard_map/cond/branch_0_fun/ppermute | solution.py:275
  8.2 0.7 %collective-permute-start.4 = (f32[6,2,256]{2,1,0:T(2,128)S(1)}, f32[6,2,256]{2,1,0:T(2,128)S(1)}, u32[]{:S(2)}, u32[]{:S(2)}) collective-permute-start(f32[6,2,256]{2,1,0:T(2,128)S(1)} %get-tuple-element.33), channel_id=1, source_target_pairs={{32,16},{48,32},{64,48},{80,64},{96,80},{160,144},{176,160},{192,1... | collective-permute-start | bytes 36872 | tf_op jit(solution)/shard_map/cond/branch_0_fun/ppermute | solution.py:246
  8.8 0.7 %collective-permute-start.8 = (f32[6,2,256]{2,1,0:T(2,128)S(1)}, f32[6,2,256]{2,1,0:T(2,128)S(1)}, u32[]{:S(2)}, u32[]{:S(2)}) collective-permute-start(f32[6,2,256]{2,1,0:T(2,128)S(1)} %get-tuple-element.44), channel_id=1, source_target_pairs={{16,32},{32,48},{48,64},{64,80},{80,96},{144,160},{160,176},{176,1... | collective-permute-start | bytes 36872 | tf_op jit(solution)/shard_map/cond/branch_0_fun/ppermute | solution.py:246
  9.5 0.0 collective-permute-done.3
  9.5 0.0 collective-permute-done.4
  9.5 0.4 %edges_z.2 = (f32[2,384]{1,0:T(2,128)S(1)}, f32[2,384]{1,0:T(2,128)S(1)}) custom-call(f32[6,64,256]{2,1,0:T(8,128)S(1)} %get-tuple-element.34.u_ref), custom_call_target="tpu_custom_call" | custom-call | tf_op jit(solution)/shard_map/cond/branch_0_fun/edges_z/pallas_call | solution.py:163
  10.0 9.7 %collective-permute-start.5 = (f32[2,384]{1,0:T(2,128)S(1)}, f32[2,384]{1,0:T(2,128)S(1)}, u32[]{:S(2)}, u32[]{:S(2)}) collective-permute-start(f32[2,384]{1,0:T(2,128)S(1)} %get-tuple-element.36), channel_id=1, source_target_pairs={{0,15},{1,0},{2,1},{3,2},{4,3},{5,4},{6,5},{7,6},{8,7},{9,8},{10,9... | collective-permute-start | bytes 9224 | tf_op jit(solution)/shard_map/cond/branch_0_fun/ppermute | solution.py:242
  19.7 0.0 collective-permute-start.6
  19.7 0.7 %collective-permute-start.7 = (f32[6,2,256]{2,1,0:T(2,128)S(1)}, f32[6,2,256]{2,1,0:T(2,128)S(1)}, u32[]{:S(2)}, u32[]{:S(2)}) collective-permute-start(f32[6,2,256]{2,1,0:T(2,128)S(1)} %get-tuple-element.42), channel_id=1, source_target_pairs={{0,16},{16,0}} | collective-permute-start | bytes 36872 | tf_op jit(solution)/shard_map/cond/branch_0_fun/ppermute | solution.py:281
  20.4 1.0 %local_parts.2 = (f32[6,64,256]{2,1,0:T(8,128)S(1)}, f32[6,64,256]{2,1,0:T(8,128)S(1)}) custom-call(f32[6,64,256]{2,1,0:T(8,128)S(1)} %get-tuple-element.34.u_ref), custom_call_target="tpu_custom_call" | custom-call | flops 1000000000 | bytes 1179648 | tf_op jit(solution)/shard_map/cond/branch_0_fun/local_parts/pallas_call | solution.py:186
  21.4 0.0 collective-permute-done.5.high_ref
  21.4 0.0 collective-permute-done.6.low_ref
  21.4 0.4 %join_z.2 = f32[6,64,256]{2,1,0:T(8,128)S(1)} custom-call(f32[6,64,256]{2,1,0:T(8,128)S(1)} %get-tuple-element.35.local_ref, f32[2,384]{1,0:T(2,128)S(1)} %collective-permute-done.5.high_ref, f32[2,384]{1,0:T(2,128)S(1)} %collective-permute-done.6.low_ref), custom_call_target="tpu_custom_call" | custom-call | tf_op jit(solution)/shard_map/cond/branch_0_fun/join_z/pallas_call | solution.py:215
  21.8 0.0 collective-permute-done.8
  21.9 0.0 collective-permute-done.7
  21.9 2.8 %collective-permute-start.10 = (f32[6,2,256]{2,1,0:T(2,128)S(1)}, f32[6,2,256]{2,1,0:T(2,128)S(1)}, u32[]{:S(2)}, u32[]{:S(2)}) collective-permute-start(f32[6,2,256]{2,1,0:T(2,128)S(1)} %get-tuple-element.92), channel_id=1, source_target_pairs={{128,112},{256,240},{384,368},{512,496},{640,624},{768,752},{896,8... | collective-permute-start | bytes 36872 | tf_op jit(solution)/shard_map/ppermute | solution.py:246
  24.7 0.0 copy-start
  24.7 0.0 collective-permute-done.9.wrap_ref
  24.8 0.9 %join_y.1.made_hbm = f32[6,64,256]{2,1,0:T(8,128)} custom-call(f32[6,64,256]{2,1,0:T(8,128)S(1)} %get-tuple-element.87.local_ref, f32[6,2,256]{2,1,0:T(2,128)S(1)} %collective-permute-done.9.wrap_ref, f32[6,2,256]{2,1,0:T(2,128)S(1)} %get-tuple-element.89.low_ref, f32[6,2,256]{2,1,0:T(2,128)S(1)} %get-tuple-element.109.high_ref.low_ref), custom_call_target="tpu_custom_call" | custom-call | flops 589824 | bytes 786432 | tf_op jit(solution)/shard_map/join_y/pallas_call | solution.py:118
  25.7 0.0 copy-done
  25.7 0.0 collective-permute-done.10.wrap_ref
  25.7 0.1 join_y_last.1
  (3 shorter events, 0.0 us)
Async XLA Ops:
  1.7 23.0 %collective-permute-start.9 = (f32[6,2,256]{2,1,0:T(2,128)S(1)}, f32[6,2,256]{2,1,0:T(2,128)S(1)}, u32[]{:S(2)}, u32[]{:S(2)}) collective-permute-start(f32[6,2,256]{2,1,0:T(2,128)S(1)} %get-tuple-element.88), channel_id=1, source_target_pairs={{112,128},{240,256},{368,384},{496,512},{624,640},{752,768},{880,8... | collective-permute-start | bytes 36872 | tf_op jit(solution)/shard_map/ppermute | solution.py:246
  3.0 6.5 %collective-permute-start.3 = (f32[6,2,256]{2,1,0:T(2,128)S(1)}, f32[6,2,256]{2,1,0:T(2,128)S(1)}, u32[]{:S(2)}, u32[]{:S(2)}) collective-permute-start(f32[6,2,256]{2,1,0:T(2,128)S(1)} %get-tuple-element.42), channel_id=1, source_target_pairs={{1,17},{2,18},{3,19},{4,20},{5,21},{6,22},{7,23},{8,24},{9,25},{10... | collective-permute-start | bytes 36872 | tf_op jit(solution)/shard_map/cond/branch_0_fun/ppermute | solution.py:275
  8.2 1.4 %collective-permute-start.4 = (f32[6,2,256]{2,1,0:T(2,128)S(1)}, f32[6,2,256]{2,1,0:T(2,128)S(1)}, u32[]{:S(2)}, u32[]{:S(2)}) collective-permute-start(f32[6,2,256]{2,1,0:T(2,128)S(1)} %get-tuple-element.33), channel_id=1, source_target_pairs={{32,16},{48,32},{64,48},{80,64},{96,80},{160,144},{176,160},{192,1... | collective-permute-start | bytes 36872 | tf_op jit(solution)/shard_map/cond/branch_0_fun/ppermute | solution.py:246
  8.8 13.0 %collective-permute-start.8 = (f32[6,2,256]{2,1,0:T(2,128)S(1)}, f32[6,2,256]{2,1,0:T(2,128)S(1)}, u32[]{:S(2)}, u32[]{:S(2)}) collective-permute-start(f32[6,2,256]{2,1,0:T(2,128)S(1)} %get-tuple-element.44), channel_id=1, source_target_pairs={{16,32},{32,48},{48,64},{64,80},{80,96},{144,160},{160,176},{176,1... | collective-permute-start | bytes 36872 | tf_op jit(solution)/shard_map/cond/branch_0_fun/ppermute | solution.py:246
  10.0 11.4 %collective-permute-start.5 = (f32[2,384]{1,0:T(2,128)S(1)}, f32[2,384]{1,0:T(2,128)S(1)}, u32[]{:S(2)}, u32[]{:S(2)}) collective-permute-start(f32[2,384]{1,0:T(2,128)S(1)} %get-tuple-element.36), channel_id=1, source_target_pairs={{0,15},{1,0},{2,1},{3,2},{4,3},{5,4},{6,5},{7,6},{8,7},{9,8},{10,9... | collective-permute-start | bytes 9224 | tf_op jit(solution)/shard_map/cond/branch_0_fun/ppermute | solution.py:242
  19.7 1.7 %collective-permute-start.6 = (f32[2,384]{1,0:T(2,128)S(1)}, f32[2,384]{1,0:T(2,128)S(1)}, u32[]{:S(2)}, u32[]{:S(2)}) collective-permute-start(f32[2,384]{1,0:T(2,128)S(1)} %get-tuple-element.37), channel_id=1, source_target_pairs={{0,1},{1,2},{2,3},{3,4},{4,5},{5,6},{6,7},{7,8},{8,9},{9,10},{10,1... | collective-permute-start | bytes 9224 | tf_op jit(solution)/shard_map/cond/branch_0_fun/ppermute | solution.py:242
  19.7 2.1 %collective-permute-start.7 = (f32[6,2,256]{2,1,0:T(2,128)S(1)}, f32[6,2,256]{2,1,0:T(2,128)S(1)}, u32[]{:S(2)}, u32[]{:S(2)}) collective-permute-start(f32[6,2,256]{2,1,0:T(2,128)S(1)} %get-tuple-element.42), channel_id=1, source_target_pairs={{0,16},{16,0}} | collective-permute-start | bytes 36872 | tf_op jit(solution)/shard_map/cond/branch_0_fun/ppermute | solution.py:281
  21.9 3.8 %collective-permute-start.10 = (f32[6,2,256]{2,1,0:T(2,128)S(1)}, f32[6,2,256]{2,1,0:T(2,128)S(1)}, u32[]{:S(2)}, u32[]{:S(2)}) collective-permute-start(f32[6,2,256]{2,1,0:T(2,128)S(1)} %get-tuple-element.92), channel_id=1, source_target_pairs={{128,112},{256,240},{384,368},{512,496},{640,624},{768,752},{896,8... | collective-permute-start | bytes 36872 | tf_op jit(solution)/shard_map/ppermute | solution.py:246
  24.7 1.0 %copy-start = (f32[6,64,256]{2,1,0:T(8,128)}, f32[6,64,256]{2,1,0:T(8,128)S(1)}, u32[]{:S(2)}) copy-start(f32[6,64,256]{2,1,0:T(8,128)S(1)} %get-tuple-element.93) | copy-start | bytes 1179652

commit v6 on v5

--- a/solution.py
+++ b/solution.py
@@ -194,7 +194,7 @@
     )(u)
 
 
-def join_z_kernel(local_ref, high_ref, low_ref, out_ref):
+def join_z_kernel(local_ref, high_ref, low_ref, out_hbm, out_ref, sem):
     planes, ny, nz = local_ref.shape
     ends = jnp.concatenate([low_ref[...], high_ref[...], low_ref[...], high_ref[...]], axis=0)
     ends = jnp.transpose(ends)
@@ -208,15 +208,19 @@
         low = end[:, 0:1] * low_first + end[:, 1:2] * low_rest
         high = end[:, 2:3] * high_rest + end[:, 3:4] * high_first
         out_ref[p] = local_ref[p] + low + high
+    copy = pltpu.make_async_copy(out_ref, out_hbm, sem)
+    copy.start()
+    copy.wait()
 
 
 def join_z(local, low, high):
     here = pl.BlockSpec(memory_space=pltpu.VMEM)
     return pl.pallas_call(
         join_z_kernel,
-        out_shape=jax.ShapeDtypeStruct(local.shape, jnp.float32),
+        out_shape=pltpu.HBM(local.shape, jnp.float32),
         in_specs=[here] * 3,
-        out_specs=here,
+        out_specs=pl.BlockSpec(memory_space=pl.ANY),
+        scratch_shapes=[pltpu.VMEM(local.shape, jnp.float32), pltpu.SemaphoreType.DMA],
         compiler_params=pltpu.CompilerParams(vmem_limit_bytes=vmem),
         name="join_z",
     )(local, high, low)
@@ -229,7 +233,7 @@
 def place_z(u):
     return pl.pallas_call(
         place_kernel,
-        out_shape=jax.ShapeDtypeStruct(u.shape, u.dtype),
+        out_shape=pltpu.HBM(u.shape, u.dtype),
         in_specs=[pl.BlockSpec(memory_space=pl.ANY)],
         out_specs=pl.BlockSpec(memory_space=pl.ANY),
         compiler_params=pltpu.CompilerParams(vmem_limit_bytes=vmem),

time: 26.1 us -> 25.9 us (level)
  starting transfers between devices: 20.9 us -> 20.1 us
  Pallas kernels: 3.98 us -> 4.63 us
    ppermute x4, starting transfers between devices: 5.39 us -> 4.64 us  [linked(): return lax.ppermute(shard, 'gy', pairs)]
    pallas_call x1, Pallas kernels: 0.43 us -> 1.19 us  [join_z(): pl.pallas_call(join_z_kernel, out_shape=pltpu.HBM(local.shape, jnp.float3...]
  transfers between devices with their start and end apart: 8 -> 8, of which waited for: 0 -> 0; matrix products, arithmetic and copies ran while one was open for 0% -> 0% of each run, Pallas kernels for 11% -> 14%
where the time goes in v6:
time: 25.9 us; the launch traced here: 25.7 us
  starting transfers between devices  20.1 us (78%)
  Pallas kernels  4.63 us (18%)
  between operations  0.72 us (3%)
    ppermute x2, starting transfers between devices, shifted(): lax.ppermute(shard, axis, [(i, (i + by) % count) for i in range(count)])  9.75 us
    ppermute x1, starting transfers between devices, early(): pair_in = lax.ppermute(pair, ('gy', 'gz'), first)  5.11 us
    ppermute x4, starting transfers between devices, linked(): return lax.ppermute(shard, 'gy', pairs)  4.64 us
    pallas_call x1, Pallas kernels, join_z(): pl.pallas_call(join_z_kernel, out_shape=pltpu.HBM(local.shape, jnp.float3...  1.19 us
    pallas_call x1, Pallas kernels, edges(): pl.pallas_call(edges_kernel, out_shape=(pltpu.VMEM(u.shape, jnp.float32),...  1.08 us
    pallas_call x1, Pallas kernels, local_parts(): pl.pallas_call(local_kernel, out_shape=(out, out), in_specs=[here], out_s...  1.01 us
    pallas_call x1, Pallas kernels, join(): pl.pallas_call(join_kernel, out_shape=jax.ShapeDtypeStruct(local.shape, j...  0.84 us
    ppermute x1, starting transfers between devices, early(): pair_in = jnp.where(slow, lax.ppermute(pair, ('gy', 'gz'), last), pair_in)  0.65 us
  transfers between devices with their start and end apart: 8, of which 0 were waited for; matrix products, arithmetic and copies ran while one was open for 0% of the time, Pallas kernels for 14%

profile of v6, /device:TPU:1, one launch (start us, length us, event | category | flops | bytes accessed | tf_op | source)
XLA Modules:
  0.0 25.7 jit_solution(6229721453496072395)
XLA Ops:
  0.6 1.1 %edges_y.1 = (f32[6,64,256]{2,1,0:T(8,128)S(1)}, f32[6,2,256]{2,1,0:T(2,128)S(1)}, f32[6,2,256]{2,1,0:T(2,128)S(1)}, f32[6,2,256]{2,1,0:T(2,128)S(1)}, f32[6,2,2...) custom-call(f32[6,64,256]{2,1,0:T(8,128)} %bitcast.4), custom_call_target="tpu_custom_call" | custom-call | tf_op jit(solution)/shard_map/edges_y/pallas_call | solution.py:71
  1.7 1.3 %collective-permute-start.9 = (f32[6,2,256]{2,1,0:T(2,128)S(1)}, f32[6,2,256]{2,1,0:T(2,128)S(1)}, u32[]{:S(2)}, u32[]{:S(2)}) collective-permute-start(f32[6,2,256]{2,1,0:T(2,128)S(1)} %get-tuple-element.88), channel_id=1, source_target_pairs={{112,128},{240,256},{368,384},{496,512},{624,640},{752,768},{880,8... | collective-permute-start | bytes 36872 | tf_op jit(solution)/shard_map/ppermute | solution.py:250
  3.0 19.6 %conditional.3 = (f32[6,64,256]{2,1,0:T(8,128)}, f32[6,64,256]{2,1,0:T(8,128)S(1)}, f32[6,2,256]{2,1,0:T(2,128)S(1)}, f32[6,2,256]{2,1,0:T(2,128)S(1)}) conditional(s32[]{:T(128)} %convert_element_type.7, (f32[6,2,256]{2,1,0:T(2,128)S(1)}, f32[6,64,256]{2,1,0:T(8,128)S(1)}, f32[6,2,256]{2,1,0:T(2,128)S(1)}, s32[]{:T(128)}, s32[]{:T(128)}, ...), branch_computations={%region_0.1_spmd, %region_1.2_spmd} | conditional | flops 1000009216 | bytes 1474874 | solution.py:293
  3.0 5.1 %collective-permute-start.3 = (f32[6,2,256]{2,1,0:T(2,128)S(1)}, f32[6,2,256]{2,1,0:T(2,128)S(1)}, u32[]{:S(2)}, u32[]{:S(2)}) collective-permute-start(f32[6,2,256]{2,1,0:T(2,128)S(1)} %get-tuple-element.42), channel_id=1, source_target_pairs={{1,17},{2,18},{3,19},{4,20},{5,21},{6,22},{7,23},{8,24},{9,25},{10... | collective-permute-start | bytes 36872 | tf_op jit(solution)/shard_map/cond/branch_0_fun/ppermute | solution.py:279
  8.2 0.7 %collective-permute-start.4 = (f32[6,2,256]{2,1,0:T(2,128)S(1)}, f32[6,2,256]{2,1,0:T(2,128)S(1)}, u32[]{:S(2)}, u32[]{:S(2)}) collective-permute-start(f32[6,2,256]{2,1,0:T(2,128)S(1)} %get-tuple-element.33), channel_id=1, source_target_pairs={{32,16},{48,32},{64,48},{80,64},{96,80},{160,144},{176,160},{192,1... | collective-permute-start | bytes 36872 | tf_op jit(solution)/shard_map/cond/branch_0_fun/ppermute | solution.py:250
  8.8 0.7 %collective-permute-start.8 = (f32[6,2,256]{2,1,0:T(2,128)S(1)}, f32[6,2,256]{2,1,0:T(2,128)S(1)}, u32[]{:S(2)}, u32[]{:S(2)}) collective-permute-start(f32[6,2,256]{2,1,0:T(2,128)S(1)} %get-tuple-element.44), channel_id=1, source_target_pairs={{16,32},{32,48},{48,64},{64,80},{80,96},{144,160},{160,176},{176,1... | collective-permute-start | bytes 36872 | tf_op jit(solution)/shard_map/cond/branch_0_fun/ppermute | solution.py:250
  9.5 0.0 collective-permute-done.3
  9.5 0.0 collective-permute-done.4
  9.5 0.4 %edges_z.2 = (f32[2,384]{1,0:T(2,128)S(1)}, f32[2,384]{1,0:T(2,128)S(1)}) custom-call(f32[6,64,256]{2,1,0:T(8,128)S(1)} %get-tuple-element.34.u_ref), custom_call_target="tpu_custom_call" | custom-call | tf_op jit(solution)/shard_map/cond/branch_0_fun/edges_z/pallas_call | solution.py:163
  10.0 9.7 %collective-permute-start.5 = (f32[2,384]{1,0:T(2,128)S(1)}, f32[2,384]{1,0:T(2,128)S(1)}, u32[]{:S(2)}, u32[]{:S(2)}) collective-permute-start(f32[2,384]{1,0:T(2,128)S(1)} %get-tuple-element.36), channel_id=1, source_target_pairs={{0,15},{1,0},{2,1},{3,2},{4,3},{5,4},{6,5},{7,6},{8,7},{9,8},{10,9... | collective-permute-start | bytes 9224 | tf_op jit(solution)/shard_map/cond/branch_0_fun/ppermute | solution.py:246
  19.7 0.0 collective-permute-start.6
  19.7 0.7 %collective-permute-start.7 = (f32[6,2,256]{2,1,0:T(2,128)S(1)}, f32[6,2,256]{2,1,0:T(2,128)S(1)}, u32[]{:S(2)}, u32[]{:S(2)}) collective-permute-start(f32[6,2,256]{2,1,0:T(2,128)S(1)} %get-tuple-element.42), channel_id=1, source_target_pairs={{0,16},{16,0}} | collective-permute-start | bytes 36872 | tf_op jit(solution)/shard_map/cond/branch_0_fun/ppermute | solution.py:285
  20.4 1.0 %local_parts.2 = (f32[6,64,256]{2,1,0:T(8,128)S(1)}, f32[6,64,256]{2,1,0:T(8,128)S(1)}) custom-call(f32[6,64,256]{2,1,0:T(8,128)S(1)} %get-tuple-element.34.u_ref), custom_call_target="tpu_custom_call" | custom-call | flops 1000000000 | bytes 1179648 | tf_op jit(solution)/shard_map/cond/branch_0_fun/local_parts/pallas_call | solution.py:186
  21.4 0.0 collective-permute-done.5.high_ref
  21.4 0.0 collective-permute-done.6.low_ref
  21.4 1.2 %join_z.2 = f32[6,64,256]{2,1,0:T(8,128)} custom-call(f32[6,64,256]{2,1,0:T(8,128)S(1)} %get-tuple-element.35.local_ref, f32[2,384]{1,0:T(2,128)S(1)} %collective-permute-done.5.high_ref, f32[2,384]{1,0:T(2,128)S(1)} %collective-permute-done.6.low_ref), custom_call_target="tpu_custom_call" | custom-call | tf_op jit(solution)/shard_map/cond/branch_0_fun/join_z/pallas_call | solution.py:218
  22.6 0.0 collective-permute-done.8
  22.6 0.0 collective-permute-done.7
  22.7 2.0 %collective-permute-start.10 = (f32[6,2,256]{2,1,0:T(2,128)S(1)}, f32[6,2,256]{2,1,0:T(2,128)S(1)}, u32[]{:S(2)}, u32[]{:S(2)}) collective-permute-start(f32[6,2,256]{2,1,0:T(2,128)S(1)} %get-tuple-element.92), channel_id=1, source_target_pairs={{128,112},{256,240},{384,368},{512,496},{640,624},{768,752},{896,8... | collective-permute-start | bytes 36872 | tf_op jit(solution)/shard_map/ppermute | solution.py:250
  24.7 0.0 collective-permute-done.9.wrap_ref
  24.7 0.8 %join_y.1.made_hbm = f32[6,64,256]{2,1,0:T(8,128)} custom-call(f32[6,64,256]{2,1,0:T(8,128)S(1)} %get-tuple-element.87.local_ref, f32[6,2,256]{2,1,0:T(2,128)S(1)} %collective-permute-done.9.wrap_ref, f32[6,2,256]{2,1,0:T(2,128)S(1)} %get-tuple-element.89.low_ref, f32[6,2,256]{2,1,0:T(2,128)S(1)} %get-tuple-element.109.high_ref.low_ref), custom_call_target="tpu_custom_call" | custom-call | flops 589824 | bytes 786432 | tf_op jit(solution)/shard_map/join_y/pallas_call | solution.py:118
  25.6 0.0 collective-permute-done.10.wrap_ref
  25.6 0.1 join_y_last.1
  (3 shorter events, 0.0 us)
Async XLA Ops:
  1.7 23.0 %collective-permute-start.9 = (f32[6,2,256]{2,1,0:T(2,128)S(1)}, f32[6,2,256]{2,1,0:T(2,128)S(1)}, u32[]{:S(2)}, u32[]{:S(2)}) collective-permute-start(f32[6,2,256]{2,1,0:T(2,128)S(1)} %get-tuple-element.88), channel_id=1, source_target_pairs={{112,128},{240,256},{368,384},{496,512},{624,640},{752,768},{880,8... | collective-permute-start | bytes 36872 | tf_op jit(solution)/shard_map/ppermute | solution.py:250
  3.0 6.5 %collective-permute-start.3 = (f32[6,2,256]{2,1,0:T(2,128)S(1)}, f32[6,2,256]{2,1,0:T(2,128)S(1)}, u32[]{:S(2)}, u32[]{:S(2)}) collective-permute-start(f32[6,2,256]{2,1,0:T(2,128)S(1)} %get-tuple-element.42), channel_id=1, source_target_pairs={{1,17},{2,18},{3,19},{4,20},{5,21},{6,22},{7,23},{8,24},{9,25},{10... | collective-permute-start | bytes 36872 | tf_op jit(solution)/shard_map/cond/branch_0_fun/ppermute | solution.py:279
  8.2 1.4 %collective-permute-start.4 = (f32[6,2,256]{2,1,0:T(2,128)S(1)}, f32[6,2,256]{2,1,0:T(2,128)S(1)}, u32[]{:S(2)}, u32[]{:S(2)}) collective-permute-start(f32[6,2,256]{2,1,0:T(2,128)S(1)} %get-tuple-element.33), channel_id=1, source_target_pairs={{32,16},{48,32},{64,48},{80,64},{96,80},{160,144},{176,160},{192,1... | collective-permute-start | bytes 36872 | tf_op jit(solution)/shard_map/cond/branch_0_fun/ppermute | solution.py:250
  8.8 13.8 %collective-permute-start.8 = (f32[6,2,256]{2,1,0:T(2,128)S(1)}, f32[6,2,256]{2,1,0:T(2,128)S(1)}, u32[]{:S(2)}, u32[]{:S(2)}) collective-permute-start(f32[6,2,256]{2,1,0:T(2,128)S(1)} %get-tuple-element.44), channel_id=1, source_target_pairs={{16,32},{32,48},{48,64},{64,80},{80,96},{144,160},{160,176},{176,1... | collective-permute-start | bytes 36872 | tf_op jit(solution)/shard_map/cond/branch_0_fun/ppermute | solution.py:250
  10.0 11.4 %collective-permute-start.5 = (f32[2,384]{1,0:T(2,128)S(1)}, f32[2,384]{1,0:T(2,128)S(1)}, u32[]{:S(2)}, u32[]{:S(2)}) collective-permute-start(f32[2,384]{1,0:T(2,128)S(1)} %get-tuple-element.36), channel_id=1, source_target_pairs={{0,15},{1,0},{2,1},{3,2},{4,3},{5,4},{6,5},{7,6},{8,7},{9,8},{10,9... | collective-permute-start | bytes 9224 | tf_op jit(solution)/shard_map/cond/branch_0_fun/ppermute | solution.py:246
  19.7 1.7 %collective-permute-start.6 = (f32[2,384]{1,0:T(2,128)S(1)}, f32[2,384]{1,0:T(2,128)S(1)}, u32[]{:S(2)}, u32[]{:S(2)}) collective-permute-start(f32[2,384]{1,0:T(2,128)S(1)} %get-tuple-element.37), channel_id=1, source_target_pairs={{0,1},{1,2},{2,3},{3,4},{4,5},{5,6},{6,7},{7,8},{8,9},{9,10},{10,1... | collective-permute-start | bytes 9224 | tf_op jit(solution)/shard_map/cond/branch_0_fun/ppermute | solution.py:246
  19.7 2.9 %collective-permute-start.7 = (f32[6,2,256]{2,1,0:T(2,128)S(1)}, f32[6,2,256]{2,1,0:T(2,128)S(1)}, u32[]{:S(2)}, u32[]{:S(2)}) collective-permute-start(f32[6,2,256]{2,1,0:T(2,128)S(1)} %get-tuple-element.42), channel_id=1, source_target_pairs={{0,16},{16,0}} | collective-permute-start | bytes 36872 | tf_op jit(solution)/shard_map/cond/branch_0_fun/ppermute | solution.py:285
  22.7 2.9 %collective-permute-start.10 = (f32[6,2,256]{2,1,0:T(2,128)S(1)}, f32[6,2,256]{2,1,0:T(2,128)S(1)}, u32[]{:S(2)}, u32[]{:S(2)}) collective-permute-start(f32[6,2,256]{2,1,0:T(2,128)S(1)} %get-tuple-element.92), channel_id=1, source_target_pairs={{128,112},{256,240},{384,368},{512,496},{640,624},{768,752},{896,8... | collective-permute-start | bytes 36872 | tf_op jit(solution)/shard_map/ppermute | solution.py:250
